TPU v7x, 1024 devices: a whole 4x4x32 slice. The times are simulated.
1024 devices in a mesh: ctx: 64 (over z, core), tp: 16 (over y, x).
Axes of the slice: x: 4, y: 4, z: 32, core: 2. Of those that a mesh axis runs over, the one named last changes fastest.
Arguments:
- x_in: bfloat16 [8192, 16384], P('ctx', 'tp'), may hold values from -6 to 6
- z_in: bfloat16 [8192, 16384], P('ctx', 'tp'), may hold values from -6 to 6
- b_in: bfloat16 [8192, 2048], P('ctx', 'tp'), may hold values from -6 to 6
- c_in: bfloat16 [8192, 2048], P('ctx', 'tp'), may hold values from -6 to 6
- dt_raw: float32 [8192, 256], P('ctx', 'tp'), may hold values from -2 to 2
- dt_bias: float32 [256], P('tp'), may hold values from -5.8 to -4.2
- a_log: float32 [256], P('tp'), may hold values from -2 to 1.1
- d_skip: float32 [256], P('tp'), may hold values from 0.5 to 1.5
- conv_x: float32 [4, 16384], P(None, 'tp'), may hold values from -3 to 3
- conv_b: float32 [4, 2048], P(None, 'tp'), may hold values from -3 to 3
- conv_c: float32 [4, 2048], P(None, 'tp'), may hold values from -3 to 3
- norm_gain: float32 [16384], P('tp'), may hold values from 0.1 to 1.9
Outputs:
- mixed_out: bfloat16 [16384, 8192], P(('tp', 'ctx'))
All inputs are finite; a program needn't handle non-finite values.
Results may differ from a plain program's by a relative error of at most 0.007.
Values may be sent and summed in bfloat16 or wider, within the bound.
No kernel may reach another device: no remote copies, remote signals or barrier semaphores. Data moves between devices by JAX's collectives and lax.ppermute only.
A program may use at most 128 MiB of HBM per device.

v0:
```python
import jax
import jax.numpy as jnp
from jax import lax
from jax.sharding import PartitionSpec as P

SPAN = 128


def shifted(value, axis, steps):
    count = lax.axis_size(axis)
    initial, last = (max(0, -steps), min(count, count - steps))
    return lax.ppermute(value, axis, [(source, source + steps) for source in range(initial, last)])


def prefix(x, axis, combine, identity):
    length, place = (lax.axis_size(axis), lax.axis_index(axis))
    everything = jax.tree.map(
        lambda part, kind: lax.all_gather(part.astype(kind), axis),
        x,
        jax.tree.map(lambda a: jnp.bfloat16 if a.dtype == jnp.float32 else a.dtype, x),
    )
    start = jax.tree.map(
        lambda part, zero: jnp.broadcast_to(jnp.asarray(zero, part.dtype), part.shape), x, identity
    )

    def lap(k, before):
        reached = k < place
        new = combine(
            before, jax.tree.map(lambda part, own: part[k].astype(own.dtype), everything, x)
        )
        return jax.tree.map(lambda a, b: jnp.where(reached, a, b), new, before)

    return lax.fori_loop(0, length, lap, start)


def causal_silu(padded, taps, length):
    rows_f = padded.astype(jnp.float32)
    total = taps[0] * rows_f[0:length]
    for offset in range(1, taps.shape[0]):
        total = total + taps[offset] * rows_f[offset : offset + length]
    return jax.nn.silu(total).astype(jnp.bfloat16)


def combine(earlier, later):
    return (earlier[0] + later[0], jnp.exp(later[0])[:, None, None] * earlier[1] + later[1])


def shards(
    x_in, z_in, b_in, c_in, dt_raw, dt_bias, a_log, d_skip, conv_x, conv_b, conv_c, norm_gain
):
    length, width = x_in.shape
    heads = dt_raw.shape[1]
    head_size = width // heads
    taps = conv_x.shape[0]
    blocks = length // SPAN
    tails = shifted(
        (x_in[length - taps + 1 :], b_in[length - taps + 1 :], c_in[length - taps + 1 :]), "ctx", 1
    )
    x_act = causal_silu(jnp.concatenate([tails[0], x_in], axis=0), conv_x, length)
    b_act = causal_silu(jnp.concatenate([tails[1], b_in], axis=0), conv_b, length)
    c_act = causal_silu(jnp.concatenate([tails[2], c_in], axis=0), conv_c, length)
    delta = jax.nn.softplus(dt_raw + dt_bias)
    rates = -jnp.exp(a_log) * delta
    logs = jnp.cumsum(rates.reshape(blocks, SPAN, heads), axis=1)
    delta_blocks = delta.reshape(blocks, SPAN, heads)
    x_blocks = x_act.reshape(blocks, SPAN, heads, head_size)
    b_blocks = b_act.reshape(blocks, SPAN, -1)
    c_blocks = c_act.reshape(blocks, SPAN, -1)
    lower = jnp.tril(jnp.ones((SPAN, SPAN), dtype=bool))

    def within_block(item):
        x_part, b_part, c_part, log_part, delta_part = item
        scores = jnp.dot(c_part, b_part.T, preferred_element_type=jnp.float32)
        log_rows = log_part.T
        decay = jnp.exp(
            jnp.where(lower[None], log_rows[:, :, None] - log_rows[:, None, :], -jnp.inf)
        )
        weights = (scores[None] * decay * delta_part.T[:, None, :]).astype(jnp.bfloat16)
        return jnp.einsum("hts,shp->thp", weights, x_part, preferred_element_type=jnp.float32)

    inner = lax.map(within_block, (x_blocks, b_blocks, c_blocks, logs, delta_blocks))
    last = logs[:, -1, :]
    scaled = (
        (jnp.exp(last[:, None, :] - logs) * delta_blocks)[..., None] * x_blocks.astype(jnp.float32)
    ).astype(jnp.bfloat16)
    update = jnp.einsum("cshp,csn->chpn", scaled, b_blocks, preferred_element_type=jnp.float32)
    entering = [jnp.zeros(update.shape[1:], jnp.float32)]
    entering.append(jnp.exp(last[0])[:, None, None] * entering[-1] + update[0])
    own_total = (jnp.sum(last, axis=0), entering[blocks])
    identity = (jnp.zeros_like(own_total[0]), jnp.zeros_like(own_total[1]))
    incoming = prefix(own_total, "ctx", combine, identity)
    before = jnp.cumsum(last, axis=0) - last
    state_in = jnp.exp(before)[:, :, None, None] * incoming[1][None] + jnp.stack(entering[:blocks])
    state_low = state_in.astype(jnp.bfloat16)
    outer = jnp.einsum("ctn,chpn->cthp", c_blocks, state_low, preferred_element_type=jnp.float32)
    y_val = (
        inner + jnp.exp(logs)[..., None] * outer + d_skip[:, None] * x_blocks.astype(jnp.float32)
    )
    gated = y_val.reshape(length, width) * jax.nn.silu(z_in.astype(jnp.float32))
    meansq = jnp.mean(gated * gated, axis=-1, keepdims=True)
    normed = (gated * lax.rsqrt(meansq + 1e-05) * norm_gain).astype(jnp.bfloat16)
    return lax.all_to_all(normed.T, "ctx", split_axis=0, concat_axis=1, tiled=True)


def solution(mesh):
    return jax.shard_map(
        shards,
        mesh=mesh,
        in_specs=(
            P("ctx", "tp"),
            P("ctx", "tp"),
            P("ctx", "tp"),
            P("ctx", "tp"),
            P("ctx", "tp"),
            P("tp"),
            P("tp"),
            P("tp"),
            P(None, "tp"),
            P(None, "tp"),
            P(None, "tp"),
            P("tp"),
        ),
        out_specs=P(("tp", "ctx"), None),
        check_vma=False,
    )
```

profile of v0, /device:TPU:1, one launch (start us, length us, event | category | flops | bytes accessed | tf_op | source)
XLA Modules:
  0.0 321.5 jit_solution(14205970372313009886)
XLA Ops:
  7.5 4.9 %collective-permute-start = (bf16[3,1024]{0,1:T(8,128)(2,1)S(1)}, bf16[3,1024]{0,1:T(8,128)(2,1)S(1)}, u32[]{:S(2)}, u32[]{:S(2)}) collective-permute-start(bf16[3,1024]{0,1:T(8,128)(2,1)S(1)} %copy.57), channel_id=1, source_target_pairs={{0,16},{16,32},{32,48},{48,64},{64,80},{80,96},{96,112},{112,128},... | collective-permute-start | bytes 18440 | tf_op jit(solution)/shard_map/ppermute | solution.py:12
  13.1 1.9 collective-permute-start.2
  19.4 1.1 copy.58
  20.5 5.0 %collective-permute-done.2 = bf16[3,128]{1,0:T(4,128)(2,1)S(1)} collective-permute-done((bf16[3,128]{1,0:T(4,128)(2,1)S(1)}, bf16[3,128]{1,0:T(4,128)(2,1)S(1)}, u32[]{:S(2)}, u32[]{:S(2)}) %collective-permute-start.2) | collective-permute-done | bytes 800 | tf_op jit(solution)/shard_map/ppermute | solution.py:12
  26.6 1.2 fusion.11
  29.4 1.9 collective-permute-start.1
  32.2 61.7 %all-gather = bf16[64,1,16]{2,1,0:T(2,128)(2,1)S(1)} all-gather(bf16[1,1,16]{2,1,0:T(2,128)(2,1)S(1)} %slice.211), channel_id=2, replica_groups=mesh['ctx'=64,'tp'=16] {'ctx'}, dimensions={0}, use_global_device_ids=true | all-gather | bytes 2080 | tf_op jit(solution)/shard_map/all_gather | solution.py:18
  93.9 1.1 copy.63
  96.0 89.4 %all-gather.4.cloned.1.call-done = bf16[1024,64,128]{2,1,0:T(8,128)(2,1)} async-done(((bf16[16,64,128]{2,1,0:T(8,128)(2,1)}), bf16[1024,64,128]{2,1,0:T(8,128)(2,1)}) %all-gather.4.cloned.1.call-update) | async-done | bytes 16777232 | tf_op jit(solution)/shard_map/all_gather | solution.py:18
  185.4 72.6 %while.18 = (s32[]{:T(128)}, f32[16,64,128]{2,1,0:T(8,128)S(1)}, s32[]{:T(128)}, bf16[64,16]{1,0:T(8,128)(2,1)S(1)}, bf16[64,16,64,128]{3,2,1,0:T(8,128)(2,1)}, /*index=5*/s32[]{:T(128)}, s32[]{:T(128)}) while((s32[]{:T(128)}, f32[16,64,128]{2,1,0:T(8,128)S(1)}, s32[]{:T(128)}, bf16[64,16]{1,0:T(8,128)(2,1)S(1)}, ...), condition=%wide.region_2.3_spmd.clone, body=%wide.region_1.2_spmd.clone.sunk | while | flops 655380 | bytes 1310985 | solution.py:33
  185.4 1.1 fusion.39
  186.5 1.1 fusion.39
  187.7 1.1 fusion.39
  188.8 1.1 fusion.39
  190.0 1.1 fusion.39
  191.1 1.1 fusion.39
  192.2 1.1 fusion.39
  193.4 1.1 fusion.39
  194.5 1.1 fusion.39
  195.6 1.1 fusion.39
  196.8 1.1 fusion.39
  197.9 1.1 fusion.39
  199.0 1.1 fusion.39
  200.2 1.1 fusion.39
  201.3 1.1 fusion.39
  202.4 1.1 fusion.39
  203.6 1.1 fusion.39
  205.8 1.1 fusion.39
  207.0 1.1 fusion.39
  208.1 1.1 fusion.39
  209.2 1.1 fusion.39
  210.4 1.1 fusion.39
  211.5 1.1 fusion.39
  212.6 1.1 fusion.39
  213.8 1.1 fusion.39
  214.9 1.1 fusion.39
  216.1 1.1 fusion.39
  217.2 1.1 fusion.39
  218.3 1.1 fusion.39
  219.5 1.1 fusion.39
  220.6 1.1 fusion.39
  221.7 1.1 fusion.39
  222.9 1.1 fusion.39
  224.0 1.1 fusion.39
  225.1 1.1 fusion.39
  227.4 1.1 fusion.39
  258.3 1.2 fusion.2
  260.0 54.0 %all_to_all.19 = bf16[64,16,128]{2,1,0:T(8,128)(2,1)S(1)} all-to-all(bf16[64,16,128]{2,1,0:T(8,128)(2,1)S(1)} %bitcast.91), channel_id=1, replica_groups=mesh['ctx'=64,'tp'=16] {'ctx'}, dimensions={0} | all-to-all | bytes 524288 | tf_op jit(solution)/shard_map/all_to_all | solution.py:102
  (129 shorter events, 43.2 us)
Async XLA Ops:
  6.5 253.2 %copy-start = (f32[1024]{0:T(1024)S(1)}, f32[1024]{0:T(1024)}, u32[]{:S(2)}) copy-start(f32[1024]{0:T(1024)} %param.25) | copy-start | bytes 12292
  6.5 178.9 %all-gather.4.cloned.1.call-start = ((), (), s32[]{:S(2)}) async-start(), calls=%async_computation.1 | async-start | bytes 17039360 | tf_op jit(solution)/shard_map/all_gather | solution.py:18
  7.5 18.9 %collective-permute-start = (bf16[3,1024]{0,1:T(8,128)(2,1)S(1)}, bf16[3,1024]{0,1:T(8,128)(2,1)S(1)}, u32[]{:S(2)}, u32[]{:S(2)}) collective-permute-start(bf16[3,1024]{0,1:T(8,128)(2,1)S(1)} %copy.57), channel_id=1, source_target_pairs={{0,16},{16,32},{32,48},{48,64},{64,80},{80,96},{96,112},{112,128},... | collective-permute-start | bytes 18440 | tf_op jit(solution)/shard_map/ppermute | solution.py:12
  13.1 12.4 %collective-permute-start.2 = (bf16[3,128]{1,0:T(4,128)(2,1)S(1)}, bf16[3,128]{1,0:T(4,128)(2,1)S(1)}, u32[]{:S(2)}, u32[]{:S(2)}) collective-permute-start(bf16[3,128]{1,0:T(4,128)(2,1)S(1)} %slice.103), channel_id=1, source_target_pairs={{0,16},{16,32},{32,48},{48,64},{64,80},{80,96},{96,112},{112,128},... | collective-permute-start | bytes 2312 | tf_op jit(solution)/shard_map/ppermute | solution.py:12
  29.4 65.6 %collective-permute-start.1 = (bf16[3,128]{1,0:T(4,128)(2,1)S(1)}, bf16[3,128]{1,0:T(4,128)(2,1)S(1)}, u32[]{:S(2)}, u32[]{:S(2)}) collective-permute-start(bf16[3,128]{1,0:T(4,128)(2,1)S(1)} %slice.94), channel_id=1, source_target_pairs={{0,16},{16,32},{32,48},{48,64},{64,80},{80,96},{96,112},{112,128},... | collective-permute-start | bytes 2312 | tf_op jit(solution)/shard_map/ppermute | solution.py:12
Sparse Core Ops, SparseCore 0:
  28.9 156.4 all-gather.3
where the time goes:
time: 325 us; the launch traced here: 321 us
  blocking collectives  116 us (36%)
  waiting for transfers between devices  94.5 us (29%)
  other arithmetic  76.6 us (24%)
  between operations  13.6 us (4%)
  starting transfers between devices  8.75 us (3%)
  local copies, waits for them, and re-layouts  8 us (2%)
    all_gather x1, waiting for transfers between devices, prefix(): lax.all_gather(part.astype(kind), axis)  89.4 us
    select_n x64, other arithmetic, lap(): return jax.tree.map(lambda a, b: jnp.where(reached, a, b), new, before)  69.9 us
    all_gather x1, blocking collectives, prefix(): lax.all_gather(part.astype(kind), axis)  61.7 us
    all_to_all x1, blocking collectives, shards(): lax.all_to_all(normed.T, 'ctx', split_axis=0, concat_axis=1, tiled=True)  54 us
    ppermute x3, starting transfers between devices, shifted(): lax.ppermute(value, axis, [(source, source + steps) for source in range(i...  8.75 us
  transfers between devices with their start and end apart: 4, of which 2 were waited for; matrix products, arithmetic and copies ran while one was open for 3% of the time, Pallas kernels for 0%

commit v1 on v0

v1 whole, which is shorter than its diff:
```python
import jax
import jax.numpy as jnp
from jax import lax
from jax.sharding import PartitionSpec as P

SPAN = 128
NEAR = 8


def causal_silu(padded, taps, length):
    rows_f = padded.astype(jnp.float32)
    total = taps[0] * rows_f[0:length]
    for offset in range(1, taps.shape[0]):
        total = total + taps[offset] * rows_f[offset : offset + length]
    return jax.nn.silu(total).astype(jnp.bfloat16)


def split3(value):
    first = lax.reduce_precision(value, 8, 7)
    rest = value - first
    second = lax.reduce_precision(rest, 8, 7)
    third = rest - second
    return [part.astype(jnp.bfloat16) for part in (first, second, third)]


def with_logs(body, logs):
    rows = jnp.concatenate(split3(logs), axis=-1)
    rows = jnp.pad(rows, [(0, 0)] * (rows.ndim - 1) + [(0, 16 - rows.shape[-1])])
    rows = jnp.broadcast_to(rows[..., None], rows.shape + (body.shape[-1],))
    return jnp.concatenate([body.astype(jnp.bfloat16), rows], axis=-2)


def read_logs(message):
    parts = message[..., 128:134, :].astype(jnp.float32)
    return parts[..., 0:2, :] + parts[..., 2:4, :] + parts[..., 4:6, :]


def widen(logs):
    return jnp.repeat(jnp.exp(logs), 64, axis=-2)


def entering_states(update, last):
    count = lax.axis_size("ctx")
    groups = count // NEAR
    near = [list(range(g * NEAR, (g + 1) * NEAR)) for g in range(groups)]
    far = [[i + NEAR * g for g in range(groups)] for i in range(NEAR)]
    mine = lax.axis_index("ctx") // NEAR
    message = with_logs(update.reshape(NEAR, 128, 128), last.reshape(NEAR, 2))
    message = lax.all_to_all(message, "ctx", 0, 0, tiled=True, axis_index_groups=near)
    parts = message[:, :128].astype(jnp.float32)
    part_logs = read_logs(message)
    inside, inside_logs = [jnp.zeros((128, 128), jnp.float32)], [jnp.zeros((2, 128), jnp.float32)]
    for k in range(NEAR):
        inside.append(widen(part_logs[k]) * inside[-1] + parts[k])
        inside_logs.append(inside_logs[-1] + part_logs[k])
    totals = lax.all_gather(
        with_logs(inside[NEAR], inside_logs[NEAR][:, 0]), "ctx", axis_index_groups=far
    )
    before = jnp.zeros((128, 128), jnp.float32)
    total_logs = read_logs(totals)
    for g in range(groups - 1):
        new = widen(total_logs[g]) * before + totals[g, :128].astype(jnp.float32)
        before = jnp.where(g < mine, new, before)
    states = jnp.stack(
        [(inside[k] + widen(inside_logs[k]) * before).astype(jnp.bfloat16) for k in range(NEAR)]
    )
    states = lax.all_to_all(states, "ctx", 0, 0, tiled=True, axis_index_groups=near)
    return states.reshape(update.shape)


def shards(
    x_in, z_in, b_in, c_in, dt_raw, dt_bias, a_log, d_skip, conv_x, conv_b, conv_c, norm_gain
):
    length, width = x_in.shape
    heads = dt_raw.shape[1]
    head_size = width // heads
    state = b_in.shape[1]
    taps = conv_x.shape[0]
    count = lax.axis_size("ctx")
    tails = jnp.concatenate([v[length - taps + 1 :] for v in (x_in, b_in, c_in)], axis=1)
    tails = lax.ppermute(tails, "ctx", [(i, i + 1) for i in range(count - 1)])
    tail_x, tail_b, tail_c = jnp.split(tails, [width, width + state], axis=1)
    x_act = causal_silu(jnp.concatenate([tail_x, x_in], axis=0), conv_x, length)
    b_act = causal_silu(jnp.concatenate([tail_b, b_in], axis=0), conv_b, length)
    c_act = causal_silu(jnp.concatenate([tail_c, c_in], axis=0), conv_c, length)
    delta = jax.nn.softplus(dt_raw + dt_bias)
    rates = -jnp.exp(a_log) * delta
    lower = jnp.tril(jnp.ones((SPAN, SPAN), dtype=bool))
    logs = jnp.dot(
        lower.astype(jnp.float32), rates, precision=lax.Precision.HIGHEST,
        preferred_element_type=jnp.float32,
    )
    last = logs[-1]
    x_heads = x_act.reshape(length, heads, head_size)
    x_wide = x_heads.astype(jnp.float32)
    scaled = ((jnp.exp(last - logs) * delta)[..., None] * x_wide).astype(jnp.bfloat16)
    update = jnp.einsum("shp,sn->hpn", scaled, b_act, preferred_element_type=jnp.float32)
    state_low = entering_states(update, last)
    scores = jnp.dot(c_act, b_act.T, preferred_element_type=jnp.float32)
    log_rows = logs.T
    decay = jnp.exp(jnp.where(lower[None], log_rows[:, :, None] - log_rows[:, None, :], -jnp.inf))
    weights = (scores[None] * decay * delta.T[:, None, :]).astype(jnp.bfloat16)
    inner = jnp.einsum("hts,shp->thp", weights, x_heads, preferred_element_type=jnp.float32)
    outer = jnp.einsum("tn,hpn->thp", c_act, state_low, preferred_element_type=jnp.float32)
    y_val = inner + jnp.exp(logs)[..., None] * outer + d_skip[:, None] * x_wide
    gated = y_val.reshape(length, width) * jax.nn.silu(z_in.astype(jnp.float32))
    meansq = jnp.mean(gated * gated, axis=-1, keepdims=True)
    normed = (gated * lax.rsqrt(meansq + 1e-05) * norm_gain).astype(jnp.bfloat16)
    return lax.all_to_all(normed.T, "ctx", split_axis=0, concat_axis=1, tiled=True)


def solution(mesh):
    return jax.shard_map(
        shards,
        mesh=mesh,
        in_specs=(
            P("ctx", "tp"),
            P("ctx", "tp"),
            P("ctx", "tp"),
            P("ctx", "tp"),
            P("ctx", "tp"),
            P("tp"),
            P("tp"),
            P("tp"),
            P(None, "tp"),
            P(None, "tp"),
            P(None, "tp"),
            P("tp"),
        ),
        out_specs=P(("tp", "ctx"), None),
        check_vma=False,
    )
```

time: 325 us -> 161 us (0.50)
  waiting for transfers between devices: 94.5 us -> 26.4 us
  other arithmetic: 76.6 us -> 8.55 us
  blocking collectives: 116 us -> 95.7 us
  between operations: 13.6 us -> 0.38 us
  starting transfers between devices: 8.75 us -> 19.5 us
    all_gather x1 -> x0, waiting for transfers between devices: 89.4 us -> none  [prefix(): lax.all_gather(part.astype(kind), axis)]
    select_n x64 -> x0, other arithmetic: 69.9 us -> none  [lap(): return jax.tree.map(lambda a, b: jnp.where(reached, a, b), new, before)]
    all_gather x1, blocking collectives: 61.7 us -> 41.6 us  [entering_states(): lax.all_gather(with_logs(inside[NEAR], inside_logs[NEAR][:, 0]), 'ctx', a...]
    all_to_all x0 -> x2, waiting for transfers between devices: none -> 17 us  [the longest x1 9.38 us: entering_states(): lax.all_to_all(message, 'ctx', 0, 0, tiled=True, axis_index_groups=near)]
    all_to_all x0 -> x2, starting transfers between devices: none -> 14.4 us  [the longest x1 10 us: entering_states(): lax.all_to_all(states, 'ctx', 0, 0, tiled=True, axis_index_groups=near)]
    unnamed x1 -> x7, other arithmetic: 0.01 us -> 4.58 us
    ppermute x3 -> x1, waiting for transfers between devices: 5.05 us -> 9.46 us  [shards(): tails = lax.ppermute(tails, 'ctx', [(i, i + 1) for i in range(count - 1)])]
    ppermute x3 -> x1, starting transfers between devices: 8.75 us -> 5.07 us  [shards(): tails = lax.ppermute(tails, 'ctx', [(i, i + 1) for i in range(count - 1)])]
  transfers between devices with their start and end apart: 4 -> 3, of which waited for: 2 -> 3; matrix products, arithmetic and copies ran while one was open for 3% -> 1% of each run, Pallas kernels for 0% -> 0%
where the time goes in v1:
time: 161 us; the launch traced here: 160 us
  blocking collectives  95.7 us (59%)
  waiting for transfers between devices  26.4 us (16%)
  starting transfers between devices  19.5 us (12%)
  other arithmetic  8.55 us (5%)
  local copies, waits for them, and re-layouts  7.94 us (5%)
    all_to_all x1, blocking collectives, shards(): lax.all_to_all(normed.T, 'ctx', split_axis=0, concat_axis=1, tiled=True)  54.2 us
    all_gather x1, blocking collectives, entering_states(): lax.all_gather(with_logs(inside[NEAR], inside_logs[NEAR][:, 0]), 'ctx', a...  41.6 us
    all_to_all x1, starting transfers between devices, entering_states(): lax.all_to_all(states, 'ctx', 0, 0, tiled=True, axis_index_groups=near)  10 us
    ppermute x1, waiting for transfers between devices, shards(): tails = lax.ppermute(tails, 'ctx', [(i, i + 1) for i in range(count - 1)])  9.46 us
    all_to_all x1, waiting for transfers between devices, entering_states(): lax.all_to_all(message, 'ctx', 0, 0, tiled=True, axis_index_groups=near)  9.38 us
    all_to_all x1, waiting for transfers between devices, entering_states(): lax.all_to_all(states, 'ctx', 0, 0, tiled=True, axis_index_groups=near)  7.58 us
    ppermute x1, starting transfers between devices, shards(): tails = lax.ppermute(tails, 'ctx', [(i, i + 1) for i in range(count - 1)])  5.07 us
    unnamed x7, other arithmetic  4.58 us
  transfers between devices with their start and end apart: 3, of which 3 were waited for; matrix products, arithmetic and copies ran while one was open for 1% of the time, Pallas kernels for 0%

profile of v1, /device:TPU:1, one launch (start us, length us, event | category | flops | bytes accessed | tf_op | source)
XLA Modules:
  0.0 159.8 jit_solution(10755541677890046823)
XLA Ops:
  0.0 0.7 slice.213
  0.7 0.7 slice.214
  1.4 0.7 slice.215
  2.1 0.3 copy.31
  2.4 5.1 %collective-permute-start = (bf16[3,1280]{0,1:T(8,128)(2,1)S(1)}, bf16[3,1280]{0,1:T(8,128)(2,1)S(1)}, u32[]{:S(2)}, u32[]{:S(2)}) collective-permute-start(bf16[3,1280]{0,1:T(8,128)(2,1)S(1)} %copy.31), channel_id=1, source_target_pairs={{0,16},{16,32},{32,48},{48,64},{64,80},{80,96},{96,112},{112,128},... | collective-permute-start | bytes 23048 | tf_op jit(solution)/shard_map/ppermute | solution.py:81
  7.5 0.2 fusion.74
  7.7 0.2 slice_reduce_fusion
  8.0 0.1 fusion.93
  8.1 0.1 reshape_squeeze.3
  8.1 0.5 copy-done.4
  8.7 0.7 copy-done.7
  9.4 0.1 fusion.82
  9.5 0.2 copy.32
  9.6 9.5 %collective-permute-done = bf16[3,1280]{0,1:T(8,128)(2,1)S(1)} collective-permute-done((bf16[3,1280]{0,1:T(8,128)(2,1)S(1)}, bf16[3,1280]{0,1:T(8,128)(2,1)S(1)}, u32[]{:S(2)}, u32[]{:S(2)}) %collective-permute-start) | collective-permute-done | bytes 7712 | tf_op jit(solution)/shard_map/ppermute | solution.py:81
  19.2 0.7 copy-done.2
  19.9 0.2 maximum_convert_fusion
  20.2 1.2 multiply_convert_fusion.3
  21.5 0.2 convolution_convert_fusion
  21.7 0.1 broadcast_in_dim.106
  21.8 0.7 pad_maximum_fusion
  22.5 4.4 %all-to-all-start = ((bf16[8,144,128]{2,1,0:T(8,128)(2,1)}), bf16[8,144,128]{2,1,0:T(8,128)(2,1)S(1)}, u32[]{:S(2)}, u32[]{:S(2)}) async-start(bf16[8,144,128]{2,1,0:T(8,128)(2,1)} %pad_maximum_fusion), calls=%async_computation | async-start | bytes 589824 | tf_op jit(solution)/shard_map/all_to_all | solution.py:49
  26.9 9.4 %all-to-all-done = bf16[8,144,128]{2,1,0:T(8,128)(2,1)S(1)} async-done(((bf16[8,144,128]{2,1,0:T(8,128)(2,1)}), bf16[8,144,128]{2,1,0:T(8,128)(2,1)S(1)}, u32[]{:S(2)}, u32[]{:S(2)}) %all-to-all-start) | async-done | bytes 294944 | tf_op jit(solution)/shard_map/all_to_all | solution.py:49
  36.4 0.1 slice_reduce_fusion.1
  36.5 0.1 select_maximum_fusion
  36.7 0.1 pad_maximum_fusion.1
  36.8 41.6 %all-gather = bf16[1152,128]{1,0:T(8,128)(2,1)S(1)} all-gather(bf16[144,128]{1,0:T(8,128)(2,1)S(1)} %pad_maximum_fusion.1), channel_id=2, replica_groups={{0,128,256,384,512,640,768,896},{16,144,272,400,528,656,784,912},{32,16..., dimensions={0}, use_global_device_ids=true | all-gather | bytes 331776 | tf_op jit(solution)/shard_map/all_gather | solution.py:56
  78.5 0.7 convert_dynamic-update-slice_fusion
  79.2 0.6 fusion.71
  79.8 0.6 fusion.65
  80.5 0.6 fusion.66
  81.2 0.7 fusion.67
  81.8 0.6 fusion.68
  82.5 0.6 fusion.69
  83.2 0.7 fusion.70
  83.8 10.0 %all-to-all-start.1 = ((bf16[8,128,128]{2,1,0:T(8,128)(2,1)}), bf16[8,128,128]{2,1,0:T(8,128)(2,1)S(1)}, u32[]{:S(2)}, u32[]{:S(2)}) async-start(bf16[8,128,128]{2,1,0:T(8,128)(2,1)} %fusion.70), calls=%async_computation.1 | async-start | bytes 524288 | tf_op jit(solution)/shard_map/all_to_all | solution.py:67
  93.9 0.2 copy.35
  94.1 0.5 copy-done.8
  94.6 0.2 copy-done.3
  94.9 0.1 fusion.98
  95.0 7.6 %all-to-all-done.1 = bf16[8,128,128]{2,1,0:T(8,128)(2,1)S(1)} async-done(((bf16[8,128,128]{2,1,0:T(8,128)(2,1)}), bf16[8,128,128]{2,1,0:T(8,128)(2,1)S(1)}, u32[]{:S(2)}, u32[]{:S(2)}) %all-to-all-start.1) | async-done | bytes 262176 | tf_op jit(solution)/shard_map/all_to_all | solution.py:67
  102.6 0.2 convolution_multiply_fusion
  102.8 0.6 copy-done.11
  103.5 0.6 fusion.1
  104.0 0.2 multiply_reduce_fusion
  104.3 0.5 copy-done.6
  104.7 0.2 multiply_convert_fusion.2
  104.9 54.2 %all_to_all.29 = bf16[64,16,128]{2,1,0:T(8,128)(2,1)S(1)} all-to-all(bf16[64,16,128]{2,1,0:T(8,128)(2,1)S(1)} %bitcast.415), channel_id=1, replica_groups=mesh['ctx'=64,'tp'=16] {'ctx'}, dimensions={0} | all-to-all | bytes 524288 | tf_op jit(solution)/shard_map/all_to_all | solution.py:109
  159.1 0.7 copy_bitcast_fusion
  (66 shorter events, 0.8 us)
Async XLA Ops:
  2.1 5.4 %copy-start.10 = (f32[16]{0:T(128)S(1)}, f32[16]{0:T(128)}, u32[]{:S(2)}) copy-start(f32[16]{0:T(128)} %param.18) | copy-start | bytes 196
  2.1 5.4 %copy-start.5 = (f32[128,16]{0,1:T(8,128)S(1)}, f32[128,16]{0,1:T(8,128)}, u32[]{:S(2)}) copy-start(f32[128,16]{0,1:T(8,128)} %param.16) | copy-start | bytes 24580
  2.1 7.3 %copy-start = (bf16[128,1024]{1,0:T(8,128)(2,1)S(1)}, bf16[128,1024]{1,0:T(8,128)(2,1)}, u32[]{:S(2)}) copy-start(bf16[128,1024]{1,0:T(8,128)(2,1)} %param.12) | copy-start | bytes 786436
  2.4 5.1 %copy-start.9 = (f32[16]{0:T(128)S(1)}, f32[16]{0:T(128)}, u32[]{:S(2)}) copy-start(f32[16]{0:T(128)} %param.17) | copy-start | bytes 196
  2.4 16.7 %collective-permute-start = (bf16[3,1280]{0,1:T(8,128)(2,1)S(1)}, bf16[3,1280]{0,1:T(8,128)(2,1)S(1)}, u32[]{:S(2)}, u32[]{:S(2)}) collective-permute-start(bf16[3,1280]{0,1:T(8,128)(2,1)S(1)} %copy.31), channel_id=1, source_target_pairs={{0,16},{16,32},{32,48},{48,64},{64,80},{80,96},{96,112},{112,128},... | collective-permute-start | bytes 23048 | tf_op jit(solution)/shard_map/ppermute | solution.py:81
  8.0 0.7 copy-start.4
  8.7 0.7 copy-start.7
  19.1 0.8 copy-start.2
  22.5 13.8 %all-to-all-start = ((bf16[8,144,128]{2,1,0:T(8,128)(2,1)}), bf16[8,144,128]{2,1,0:T(8,128)(2,1)S(1)}, u32[]{:S(2)}, u32[]{:S(2)}) async-start(bf16[8,144,128]{2,1,0:T(8,128)(2,1)} %pad_maximum_fusion), calls=%async_computation | async-start | bytes 589824 | tf_op jit(solution)/shard_map/all_to_all | solution.py:49
  83.8 10.0 %copy-start.1 = (bf16[128,1024]{1,0:T(8,128)(2,1)S(1)}, bf16[128,1024]{1,0:T(8,128)(2,1)}, u32[]{:S(2)}) copy-start(bf16[128,1024]{1,0:T(8,128)(2,1)} %param.13) | copy-start | bytes 786436
  83.8 18.8 %all-to-all-start.1 = ((bf16[8,128,128]{2,1,0:T(8,128)(2,1)}), bf16[8,128,128]{2,1,0:T(8,128)(2,1)S(1)}, u32[]{:S(2)}, u32[]{:S(2)}) async-start(bf16[8,128,128]{2,1,0:T(8,128)(2,1)} %fusion.70), calls=%async_computation.1 | async-start | bytes 524288 | tf_op jit(solution)/shard_map/all_to_all | solution.py:67
  93.9 0.7 copy-start.8
  94.0 0.8 copy-start.3
  102.8 0.7 copy-start.11
  104.0 0.7 copy-start.6

commit v2 on v1

v2 whole, which is shorter than its diff:
```python
import jax
import jax.numpy as jnp
from jax import lax
from jax.experimental import pallas as pl
from jax.experimental.pallas import tpu as pltpu
from jax.sharding import PartitionSpec as P

SPAN = 128
NEAR = 8
EXTRA = 16
LOW = 20 << 20


def split3(value):
    first = value.astype(jnp.bfloat16)
    rest = value - first.astype(jnp.float32)
    second = rest.astype(jnp.bfloat16)
    third = (rest - second.astype(jnp.float32)).astype(jnp.bfloat16)
    return [first, second, third]


def pack_tails(x_ref, b_ref, c_ref, out_ref):
    width, state = x_ref.shape[1], b_ref.shape[1]
    out_ref[:, :width] = x_ref[...]
    out_ref[:, width : width + state] = b_ref[...]
    out_ref[:, width + state :] = c_ref[...]


def conv_silu(tail, rows, taps, scratch):
    length, width = rows.shape
    back = taps.shape[0] - 1
    scratch[0:8, :width] = tail[8:16].astype(jnp.float32)
    scratch[8 : 8 + length, :width] = rows.astype(jnp.float32)
    total = taps[0:1] * scratch[8 - back : 8 - back + length, :width]
    for k in range(1, back + 1):
        total = total + taps[k : k + 1] * scratch[8 - back + k : 8 - back + k + length, :width]
    return (total / (1.0 + jnp.exp(-total))).astype(jnp.bfloat16)


def local_part(
    tail_ref, x_ref, b_ref, c_ref, dt_ref, bias_ref, alog_ref, tx_ref, tb_ref, tc_ref,
    message_ref, x_out, b_out, c_out, logs_out, delta_out, scratch,
):
    length, width = x_ref.shape
    state = b_ref.shape[1]
    heads = dt_ref.shape[0]
    b_act = conv_silu(tail_ref[:, width : width + state], b_ref[...], tb_ref[...], scratch)
    b_out[...] = b_act
    c_out[...] = conv_silu(tail_ref[:, width + state :], c_ref[...], tc_ref[...], scratch)
    raw = dt_ref[...] + bias_ref[...].T
    grown = jnp.exp(-jnp.abs(raw))
    one_more = 1.0 + grown
    ratio = grown / jnp.where(one_more == 1.0, 1.0, one_more - 1.0)
    delta = jnp.maximum(raw, 0.0) + jnp.where(one_more == 1.0, grown, jnp.log(one_more) * ratio)
    rates = -jnp.exp(alog_ref[...].T) * delta
    until = (
        lax.broadcasted_iota(jnp.int32, (length, length), 0)
        <= lax.broadcasted_iota(jnp.int32, (length, length), 1)
    ).astype(jnp.bfloat16)
    logs = jnp.zeros(rates.shape, jnp.float32)
    for part in split3(rates):
        logs = logs + jnp.dot(part, until, preferred_element_type=jnp.float32)
    last = logs[:, length - 1 : length]
    logs_out[...] = logs
    delta_out[...] = delta
    scale = (jnp.exp(last - logs) * delta).T
    decay = [part.astype(jnp.float32) for part in split3(jnp.exp(last))]
    lane = lax.broadcasted_iota(jnp.int32, (length, 128), 1)
    row = lax.broadcasted_iota(jnp.int32, (EXTRA, 128), 0)
    for p in range(width // 128):
        here = slice(128 * p, 128 * p + 128)
        x_act = conv_silu(tail_ref[:, here], x_ref[:, here], tx_ref[:, here], scratch)
        x_out[:, here] = x_act
        factor = jnp.where(lane < 64, scale[:, 2 * p : 2 * p + 1], scale[:, 2 * p + 1 : 2 * p + 2])
        scaled = (factor * x_act.astype(jnp.float32)).astype(jnp.bfloat16)
        update = lax.dot_general(
            scaled, b_act, (((0,), (0,)), ((), ())), preferred_element_type=jnp.float32
        )
        message_ref[p, 0:128, :] = update.astype(jnp.bfloat16)
        extra = jnp.zeros((EXTRA, 128), jnp.float32)
        for k in range(6):
            h = 2 * p + k % 2
            extra = jnp.where(row == k, decay[k // 2][h : h + 1, :], extra)
        message_ref[p, 128 : 128 + EXTRA, :] = extra.astype(jnp.bfloat16)


def read_decays(message):
    parts = message[..., 128:134, :].astype(jnp.float32)
    return parts[..., 0:2, :] + parts[..., 2:4, :] + parts[..., 4:6, :]


def widen(decay):
    return jnp.repeat(decay, 64, axis=-2)


def entering_states(message):
    count = lax.axis_size("ctx")
    groups = count // NEAR
    near = [list(range(g * NEAR, (g + 1) * NEAR)) for g in range(groups)]
    message = lax.all_to_all(message, "ctx", 0, 0, tiled=True, axis_index_groups=near)
    parts = message[:, :128].astype(jnp.float32)
    part_decays = read_decays(message)
    inside, decays = [jnp.zeros((128, 128), jnp.float32)], [jnp.ones((2, 128), jnp.float32)]
    for k in range(NEAR):
        inside.append(widen(part_decays[k]) * inside[-1] + parts[k])
        decays.append(decays[-1] * part_decays[k])
    total, decay = inside[NEAR], widen(decays[NEAR])
    before = jnp.zeros((128, 128), jnp.float32)
    came = jnp.zeros((128, 128), jnp.bfloat16)
    for g in range(groups - 1):
        on = (decay * came.astype(jnp.float32) + total).astype(jnp.bfloat16)
        came = lax.ppermute(on, "ctx", [(i, i + NEAR) for i in near[g]])
        before = before + came.astype(jnp.float32)
    inside = lax.optimization_barrier(jnp.stack(inside[:NEAR]))
    decays = lax.optimization_barrier(jnp.stack(decays[:NEAR]))
    states = (inside + widen(decays) * before).astype(jnp.bfloat16)
    states = lax.all_to_all(states, "ctx", 0, 0, tiled=True, axis_index_groups=near)
    return states.reshape(NEAR * 128, 128)


def shards(
    x_in, z_in, b_in, c_in, dt_raw, dt_bias, a_log, d_skip, conv_x, conv_b, conv_c, norm_gain
):
    length, width = x_in.shape
    heads = dt_raw.shape[1]
    head_size = width // heads
    state = b_in.shape[1]
    count = lax.axis_size("ctx")
    whole = width + 2 * state
    f32, bf16 = jnp.float32, jnp.bfloat16
    end = length // 16 - 1
    tails = pl.pallas_call(
        pack_tails,
        grid=(1,),
        in_specs=[pl.BlockSpec((16, v), lambda i: (end, 0)) for v in (width, state, state)],
        out_specs=pl.BlockSpec((16, whole), lambda i: (0, 0)),
        out_shape=jax.ShapeDtypeStruct((16, whole), bf16),
        name="pack_tails",
    )(x_in, b_in, c_in)
    tails = lax.ppermute(tails, "ctx", [(i, i + 1) for i in range(count - 1)])
    message, x_act, b_act, c_act, logs, delta = pl.pallas_call(
        local_part,
        out_shape=[
            jax.ShapeDtypeStruct((width // 128, 128 + EXTRA, state), bf16),
            jax.ShapeDtypeStruct((length, width), bf16),
            jax.ShapeDtypeStruct((length, state), bf16),
            jax.ShapeDtypeStruct((length, state), bf16),
            jax.ShapeDtypeStruct((heads, length), f32),
            jax.ShapeDtypeStruct((heads, length), f32),
        ],
        scratch_shapes=[pltpu.VMEM((8 + length, 128), f32)],
        compiler_params=pltpu.CompilerParams(vmem_limit_bytes=LOW),
        name="local_part",
    )(
        tails, x_in, b_in, c_in, dt_raw.T, dt_bias[None], a_log[None], conv_x, conv_b, conv_c
    )
    lower = jnp.triu(jnp.ones((SPAN, SPAN), dtype=bool))
    x_heads = x_act.T.reshape(heads, head_size, length)
    scores = jnp.dot(b_act, c_act.T, preferred_element_type=f32)
    decay = jnp.exp(jnp.where(lower[None], logs[:, None, :] - logs[:, :, None], -jnp.inf))
    weights = (scores[None] * decay * delta[:, :, None]).astype(bf16)
    inner = jnp.einsum("hst,hps->hpt", weights, x_heads, preferred_element_type=f32)
    inner = inner + d_skip[:, None, None] * x_heads.astype(f32)
    gate = jax.nn.silu(z_in.astype(f32)).T
    gain = gate * norm_gain[:, None]
    inner, gate, gain, grown = lax.optimization_barrier((inner, gate, gain, jnp.exp(logs)))
    state_low = entering_states(message)
    outer = jnp.dot(state_low, c_act.T, preferred_element_type=f32)
    y_val = inner + grown[:, None, :] * outer.reshape(heads, head_size, length)
    y_val = y_val.reshape(width, length)
    gated = y_val * gate
    meansq = jnp.mean(gated * gated, axis=0, keepdims=True)
    normed = (y_val * gain * lax.rsqrt(meansq + 1e-05)).astype(bf16)
    return lax.all_to_all(normed, "ctx", split_axis=0, concat_axis=1, tiled=True)


def solution(mesh):
    return jax.shard_map(
        shards,
        mesh=mesh,
        in_specs=(
            P("ctx", "tp"),
            P("ctx", "tp"),
            P("ctx", "tp"),
            P("ctx", "tp"),
            P("ctx", "tp"),
            P("tp"),
            P("tp"),
            P("tp"),
            P(None, "tp"),
            P(None, "tp"),
            P(None, "tp"),
            P("tp"),
        ),
        out_specs=P(("tp", "ctx"), None),
        check_vma=False,
    )
```

time: 161 us -> 142 us (0.88)
  blocking collectives: 95.7 us -> 82.6 us
  other arithmetic: 8.55 us -> 1.93 us
  local copies, waits for them, and re-layouts: 7.94 us -> 3 us
  Pallas kernels: 0 us -> 3.5 us
    all_gather x1 -> x0, blocking collectives: 41.6 us -> none  [entering_states(): lax.all_gather(with_logs(inside[NEAR], inside_logs[NEAR][:, 0]), 'ctx', a...]
    all_to_all x1, blocking collectives: 54.2 us -> 82.6 us  [shards(): lax.all_to_all(normed, 'ctx', split_axis=0, concat_axis=1, tiled=True)]
    ppermute x0 -> x7, starting transfers between devices: none -> 6.51 us  [entering_states(): came = lax.ppermute(on, 'ctx', [(i, i + NEAR) for i in near[g]])]
    all_to_all x1, starting transfers between devices: 10 us -> 5.38 us  [entering_states(): lax.all_to_all(states, 'ctx', 0, 0, tiled=True, axis_index_groups=near)]
    unnamed x7 -> x11, other arithmetic: 4.58 us -> 0.2 us
    pallas_call x0 -> x2, Pallas kernels: none -> 3.5 us  [the longest x1 2.07 us: shards(): pl.pallas_call(local_part, out_shape=[jax.ShapeDtypeStruct((width // 128,...]
    slice x6 -> x0, local copies, waits for them, and re-layouts: 2.47 us -> none  [the longest x3 2.1 us: shards(): v[length - taps + 1:]]
    unnamed x26 -> x28, local copies, waits for them, and re-layouts: 4.04 us -> 2.06 us
  transfers between devices with their start and end apart: 3 -> 10, of which waited for: 3 -> 4; matrix products, arithmetic and copies ran while one was open for 1% -> 1% of each run, Pallas kernels for 0% -> 0%
where the time goes in v2:
time: 142 us; the launch traced here: 140 us
  blocking collectives  82.6 us (58%)
  waiting for transfers between devices  27.5 us (19%)
  starting transfers between devices  20.3 us (14%)
  Pallas kernels  3.5 us (2%)
  local copies, waits for them, and re-layouts  3 us (2%)
  other arithmetic  1.93 us (1%)
    all_to_all x1, blocking collectives, shards(): lax.all_to_all(normed, 'ctx', split_axis=0, concat_axis=1, tiled=True)  82.6 us
    ppermute x1, waiting for transfers between devices, shards(): tails = lax.ppermute(tails, 'ctx', [(i, i + 1) for i in range(count - 1)])  11.4 us
    all_to_all x1, waiting for transfers between devices, entering_states(): lax.all_to_all(message, 'ctx', 0, 0, tiled=True, axis_index_groups=near)  9.37 us
    ppermute x7, starting transfers between devices, entering_states(): came = lax.ppermute(on, 'ctx', [(i, i + NEAR) for i in near[g]])  6.51 us
    all_to_all x1, waiting for transfers between devices, entering_states(): lax.all_to_all(states, 'ctx', 0, 0, tiled=True, axis_index_groups=near)  5.78 us
    all_to_all x1, starting transfers between devices, entering_states(): lax.all_to_all(states, 'ctx', 0, 0, tiled=True, axis_index_groups=near)  5.38 us
    ppermute x1, starting transfers between devices, shards(): tails = lax.ppermute(tails, 'ctx', [(i, i + 1) for i in range(count - 1)])  4.92 us
    all_to_all x1, starting transfers between devices, entering_states(): lax.all_to_all(message, 'ctx', 0, 0, tiled=True, axis_index_groups=near)  3.48 us
  transfers between devices with their start and end apart: 10, of which 4 were waited for; matrix products, arithmetic and copies ran while one was open for 1% of the time, Pallas kernels for 0%

profile of v2, /device:TPU:1, one launch (start us, length us, event | category | flops | bytes accessed | tf_op | source)
XLA Modules:
  0.0 140.4 jit_solution(2496040996739724141)
XLA Ops:
  0.0 0.0 copy-start.3
  0.0 0.0 copy-start.4
  0.0 1.4 %pack_tails.1 = bf16[16,1280]{1,0:T(8,128)(2,1)} custom-call(bf16[128,1024]{1,0:T(8,128)(2,1)} %x_ref.3, bf16[128,128]{1,0:T(8,128)(2,1)} %b_ref.3, bf16[128,128]{1,0:T(8,128)(2,1)} %c_ref.3), custom_call_target="tpu_custom_call" | custom-call | tf_op jit(solution)/shard_map/pack_tails/pallas_call | solution.py:132
  1.5 4.9 %collective-permute-start = (bf16[16,1280]{1,0:T(8,128)(2,1)}, bf16[16,1280]{1,0:T(8,128)(2,1)S(1)}, u32[]{:S(2)}, u32[]{:S(2)}) collective-permute-start(bf16[16,1280]{1,0:T(8,128)(2,1)} %pack_tails.1), channel_id=1, source_target_pairs={{0,16},{16,32},{32,48},{48,64},{64,80},{80,96},{96,112},{112,128},... | collective-permute-start | bytes 122888 | tf_op jit(solution)/shard_map/ppermute | solution.py:140
  6.4 11.4 %collective-permute-done.tail_ref = bf16[16,1280]{1,0:T(8,128)(2,1)S(1)} collective-permute-done((bf16[16,1280]{1,0:T(8,128)(2,1)}, bf16[16,1280]{1,0:T(8,128)(2,1)S(1)}, u32[]{:S(2)}, u32[]{:S(2)}) %collective-permute-start) | collective-permute-done | bytes 40992 | tf_op jit(solution)/shard_map/ppermute | solution.py:140
  17.8 0.0 copy-done
  17.8 0.0 copy-done.1
  17.8 0.0 copy-done.2
  17.8 0.0 copy-done.3
  17.8 0.0 copy-done.4
  17.9 0.6 copy-done.6
  18.5 0.0 copy-done.5
  18.5 2.1 %local_part.1 = (bf16[8,144,128]{2,1,0:T(8,128)(2,1)}, bf16[128,1024]{1,0:T(8,128)(2,1)S(1)}, bf16[128,128]{1,0:T(8,128)(2,1)S(1)}, bf16[128,128]{1,0:T(8,128)(2...) custom-call(bf16[16,1280]{1,0:T(8,128)(2,1)S(1)} %collective-permute-done.tail_ref, bf16[128,1024]{1,0:T(8,128)(2,1)S(1)} %copy-done, ...), custom_call_target="tpu_custom_call" | custom-call | tf_op jit(solution)/shard_map/local_part/pallas_call | solution.py:141
  20.6 3.5 %all-to-all-start = ((bf16[8,144,128]{2,1,0:T(8,128)(2,1)}), bf16[8,144,128]{2,1,0:T(8,128)(2,1)S(1)}, u32[]{:S(2)}, u32[]{:S(2)}) async-start(bf16[8,144,128]{2,1,0:T(8,128)(2,1)} %get-tuple-element.22), calls=%async_computation | async-start | bytes 589824 | tf_op jit(solution)/shard_map/all_to_all | solution.py:100
  24.1 9.4 %all-to-all-done = bf16[8,144,128]{2,1,0:T(8,128)(2,1)S(1)} async-done(((bf16[8,144,128]{2,1,0:T(8,128)(2,1)}), bf16[8,144,128]{2,1,0:T(8,128)(2,1)S(1)}, u32[]{:S(2)}, u32[]{:S(2)}) %all-to-all-start) | async-done | bytes 294944 | tf_op jit(solution)/shard_map/all_to_all | solution.py:100
  33.6 0.1 fusion.19
  33.7 2.5 %collective-permute-start.1 = (bf16[128,128]{1,0:T(8,128)(2,1)S(1)}, bf16[128,128]{1,0:T(8,128)(2,1)S(1)}, u32[]{:S(2)}, u32[]{:S(2)}) collective-permute-start(bf16[128,128]{1,0:T(8,128)(2,1)S(1)} %get-tuple-element.27), channel_id=1, source_target_pairs={{0,128},{16,144},{32,160},{48,176},{64,192},{80,208},{96,224},{112... | collective-permute-start | bytes 98312 | tf_op jit(solution)/shard_map/ppermute | solution.py:112
  36.2 1.0 collective-permute-done.1
  37.2 0.7 collective-permute-start.2
  37.9 0.0 collective-permute-done.2
  38.0 0.7 collective-permute-start.3
  38.7 0.0 collective-permute-done.3
  38.7 0.7 collective-permute-start.4
  39.4 0.0 collective-permute-done.4
  39.5 0.7 collective-permute-start.5
  40.2 0.0 collective-permute-done.5
  40.2 0.7 collective-permute-start.6
  40.9 0.0 collective-permute-done.6
  41.0 0.7 collective-permute-start.7
  41.7 0.0 collective-permute-done.7
  41.7 0.8 fusion.10
  42.5 5.4 %all-to-all-start.1 = ((bf16[8,128,128]{2,1,0:T(8,128)(2,1)}), bf16[8,128,128]{2,1,0:T(8,128)(2,1)S(1)}, u32[]{:S(2)}, u32[]{:S(2)}) async-start(bf16[8,128,128]{2,1,0:T(8,128)(2,1)} %fusion.10), calls=%async_computation.1 | async-start | bytes 524288 | tf_op jit(solution)/shard_map/all_to_all | solution.py:117
  47.9 0.2 copy.21
  48.1 0.1 fusion.47
  48.2 0.0 copy-start.10
  48.2 0.1 fusion.4
  48.3 0.5 copy-done.10
  48.9 0.2 broadcast_multiply_fusion
  49.1 0.2 copy.20
  49.2 0.1 fusion.59
  49.4 0.7 copy-done.11
  50.1 0.8 convolution_add_fusion
  50.8 5.8 %all-to-all-done.1 = bf16[8,128,128]{2,1,0:T(8,128)(2,1)S(1)} async-done(((bf16[8,128,128]{2,1,0:T(8,128)(2,1)}), bf16[8,128,128]{2,1,0:T(8,128)(2,1)S(1)}, u32[]{:S(2)}, u32[]{:S(2)}) %all-to-all-start.1) | async-done | bytes 262176 | tf_op jit(solution)/shard_map/all_to_all | solution.py:117
  56.6 0.2 fusion
  56.8 0.2 fusion.8
  57.0 0.1 fusion.6
  57.1 82.6 %all_to_all.29 = bf16[64,16,128]{2,1,0:T(8,128)(2,1)S(1)} all-to-all(bf16[64,16,128]{2,1,0:T(8,128)(2,1)S(1)} %bitcast.285), channel_id=1, replica_groups=mesh['ctx'=64,'tp'=16] {'ctx'}, dimensions={0} | all-to-all | bytes 524288 | tf_op jit(solution)/shard_map/all_to_all | solution.py:174
  139.7 0.7 copy_bitcast_fusion
  (49 shorter events, 0.5 us)
Async XLA Ops:
  0.0 17.8 %copy-start = (bf16[128,1024]{1,0:T(8,128)(2,1)S(1)}, bf16[128,1024]{1,0:T(8,128)(2,1)}, u32[]{:S(2)}) copy-start(bf16[128,1024]{1,0:T(8,128)(2,1)} %x_ref.3) | copy-start | bytes 786436
  0.0 17.8 %copy-start.1 = (bf16[128,128]{1,0:T(8,128)(2,1)S(1)}, bf16[128,128]{1,0:T(8,128)(2,1)}, u32[]{:S(2)}) copy-start(bf16[128,128]{1,0:T(8,128)(2,1)} %b_ref.3) | copy-start | bytes 98308
  0.0 17.8 %copy-start.2 = (bf16[128,128]{1,0:T(8,128)(2,1)S(1)}, bf16[128,128]{1,0:T(8,128)(2,1)}, u32[]{:S(2)}) copy-start(bf16[128,128]{1,0:T(8,128)(2,1)} %c_ref.3) | copy-start | bytes 98308
  0.0 17.8 %copy-start.3 = (f32[4,1024]{1,0:T(4,128)S(1)}, f32[4,1024]{1,0:T(4,128)}, u32[]{:S(2)}) copy-start(f32[4,1024]{1,0:T(4,128)} %tx_ref.1) | copy-start | bytes 49156
  0.0 17.8 %copy-start.4 = (f32[128,16]{0,1:T(8,128)S(1)}, f32[128,16]{0,1:T(8,128)}, u32[]{:S(2)}) copy-start(f32[128,16]{0,1:T(8,128)} %param.16) | copy-start | bytes 24580
  1.5 16.3 %collective-permute-start = (bf16[16,1280]{1,0:T(8,128)(2,1)}, bf16[16,1280]{1,0:T(8,128)(2,1)S(1)}, u32[]{:S(2)}, u32[]{:S(2)}) collective-permute-start(bf16[16,1280]{1,0:T(8,128)(2,1)} %pack_tails.1), channel_id=1, source_target_pairs={{0,16},{16,32},{32,48},{48,64},{64,80},{80,96},{96,112},{112,128},... | collective-permute-start | bytes 122888 | tf_op jit(solution)/shard_map/ppermute | solution.py:140
  17.8 0.7 copy-start.6
  17.8 0.7 copy-start.5
  17.8 0.7 copy-start.7
  17.8 0.7 copy-start.8
  20.6 12.9 %all-to-all-start = ((bf16[8,144,128]{2,1,0:T(8,128)(2,1)}), bf16[8,144,128]{2,1,0:T(8,128)(2,1)S(1)}, u32[]{:S(2)}, u32[]{:S(2)}) async-start(bf16[8,144,128]{2,1,0:T(8,128)(2,1)} %get-tuple-element.22), calls=%async_computation | async-start | bytes 589824 | tf_op jit(solution)/shard_map/all_to_all | solution.py:100
  33.7 3.5 %collective-permute-start.1 = (bf16[128,128]{1,0:T(8,128)(2,1)S(1)}, bf16[128,128]{1,0:T(8,128)(2,1)S(1)}, u32[]{:S(2)}, u32[]{:S(2)}) collective-permute-start(bf16[128,128]{1,0:T(8,128)(2,1)S(1)} %get-tuple-element.27), channel_id=1, source_target_pairs={{0,128},{16,144},{32,160},{48,176},{64,192},{80,208},{96,224},{112... | collective-permute-start | bytes 98312 | tf_op jit(solution)/shard_map/ppermute | solution.py:112
  37.2 0.7 collective-permute-start.2
  38.0 0.7 collective-permute-start.3
  38.7 0.7 collective-permute-start.4
  39.5 0.7 collective-permute-start.5
  40.2 0.7 collective-permute-start.6
  41.0 0.7 collective-permute-start.7
  42.5 5.4 %copy-start.9 = (bf16[128,1024]{1,0:T(8,128)(2,1)S(1)}, bf16[128,1024]{1,0:T(8,128)(2,1)}, u32[]{:S(2)}) copy-start(bf16[128,1024]{1,0:T(8,128)(2,1)} %param.13) | copy-start | bytes 786436
  42.5 14.1 %all-to-all-start.1 = ((bf16[8,128,128]{2,1,0:T(8,128)(2,1)}), bf16[8,128,128]{2,1,0:T(8,128)(2,1)S(1)}, u32[]{:S(2)}, u32[]{:S(2)}) async-start(bf16[8,128,128]{2,1,0:T(8,128)(2,1)} %fusion.10), calls=%async_computation.1 | async-start | bytes 524288 | tf_op jit(solution)/shard_map/all_to_all | solution.py:117
  48.2 0.7 copy-start.10
  49.4 0.7 copy-start.11

commit v3 on v2

v3 whole, which is shorter than its diff:
```python
import jax
import jax.numpy as jnp
from jax import lax
from jax.experimental import pallas as pl
from jax.experimental.pallas import tpu as pltpu
from jax.sharding import PartitionSpec as P

SPAN = 128
NEAR = 8
EXTRA = 32
LOW = 20 << 20
HIGH = 56 << 20


def split3(value):
    first = value.astype(jnp.bfloat16)
    rest = value - first.astype(jnp.float32)
    second = rest.astype(jnp.bfloat16)
    third = (rest - second.astype(jnp.float32)).astype(jnp.bfloat16)
    return [first, second, third]


def pack_tails(x_ref, b_ref, c_ref, out_ref):
    width, state = x_ref.shape[1], b_ref.shape[1]
    out_ref[:, :width] = x_ref[...]
    out_ref[:, width : width + state] = b_ref[...]
    out_ref[:, width + state :] = c_ref[...]


def conv_silu(tail, rows, taps, scratch):
    length, width = rows.shape
    back = taps.shape[0] - 1
    scratch[0:8, :width] = tail.astype(jnp.float32)
    scratch[8 : 8 + length, :width] = rows.astype(jnp.float32)
    total = taps[0:1] * scratch[8 - back : 8 - back + length, :width]
    for k in range(1, back + 1):
        total = total + taps[k : k + 1] * scratch[8 - back + k : 8 - back + k + length, :width]
    return (total / (1.0 + jnp.exp(-total))).astype(jnp.bfloat16)


def without_halo(
    x_ref, b_ref, dt_ref, bias_ref, alog_ref, tx_ref, tb_ref,
    message_ref, logs_out, delta_out, scratch, b_scratch, extra,
):
    length, width = x_ref.shape
    back = tx_ref.shape[0] - 1
    nothing = jnp.zeros((8, 128), jnp.bfloat16)
    b_act = conv_silu(nothing, b_ref[...], tb_ref[...], b_scratch)
    raw = dt_ref[...] + bias_ref[...].T
    grown = jnp.exp(-jnp.abs(raw))
    one_more = 1.0 + grown
    ratio = grown / jnp.where(one_more == 1.0, 1.0, one_more - 1.0)
    delta = jnp.maximum(raw, 0.0) + jnp.where(one_more == 1.0, grown, jnp.log(one_more) * ratio)
    rates = -jnp.exp(alog_ref[...].T) * delta
    until = (
        lax.broadcasted_iota(jnp.int32, (length, length), 0)
        <= lax.broadcasted_iota(jnp.int32, (length, length), 1)
    ).astype(jnp.bfloat16)
    logs = jnp.zeros(rates.shape, jnp.float32)
    for part in split3(rates):
        logs = logs + jnp.dot(part, until, preferred_element_type=jnp.float32)
    last = logs[:, length - 1 : length]
    logs_out[...] = logs
    delta_out[...] = delta
    scale = (jnp.exp(last - logs) * delta).T
    decay = [part.astype(jnp.float32) for part in split3(jnp.exp(last))]
    lane = lax.broadcasted_iota(jnp.int32, (length, 128), 1)
    late = lax.broadcasted_iota(jnp.int32, (length, 128), 0) >= back
    extra[...] = jnp.zeros(extra.shape, jnp.float32)
    for p in range(width // 128):
        here = slice(128 * p, 128 * p + 128)
        x_act = conv_silu(nothing, x_ref[:, here], tx_ref[:, here], scratch)
        factor = jnp.where(lane < 64, scale[:, 2 * p : 2 * p + 1], scale[:, 2 * p + 1 : 2 * p + 2])
        scaled = jnp.where(late, factor * x_act.astype(jnp.float32), 0.0).astype(jnp.bfloat16)
        update = lax.dot_general(
            scaled, b_act, (((0,), (0,)), ((), ())), preferred_element_type=jnp.float32
        )
        message_ref[p, 0:128, :] = update.astype(jnp.bfloat16)
        for k in range(6):
            h = 2 * p + k % 2
            extra[k : k + 1, :] = jnp.broadcast_to(decay[k // 2][h : h + 1, :], (1, 128))
        extra[6:9, :] = scratch[8:11, :]
        extra[9:12, :] = scratch[5 + length : 8 + length, :]
        extra[12:15, :] = b_scratch[8:11, :]
        extra[15:18, :] = b_scratch[5 + length : 8 + length, :]
        for k, part in enumerate(split3(factor[0:8])):
            extra[18 + 3 * k : 21 + 3 * k, :] = part.astype(jnp.float32)[0:3]
        message_ref[p, 128 : 128 + EXTRA, :] = extra[...].astype(jnp.bfloat16)


def all_rows(
    tail_ref, x_ref, b_ref, c_ref, tx_ref, tb_ref, tc_ref, x_out, b_out, c_out, scratch
):
    width, state = x_ref.shape[1], b_ref.shape[1]
    for p in range(width // 128):
        here = slice(128 * p, 128 * p + 128)
        x_out[:, here] = conv_silu(tail_ref[8:16, here], x_ref[:, here], tx_ref[:, here], scratch)
    b_out[...] = conv_silu(
        tail_ref[8:16, width : width + state], b_ref[...], tb_ref[...], scratch
    )
    c_out[...] = conv_silu(tail_ref[8:16, width + state :], c_ref[...], tc_ref[...], scratch)


def widen(decay):
    return jnp.repeat(decay, 64, axis=-2)


def own_taps(first, taps):
    return sum(
        jnp.pad(taps[k] * first[..., : k, :], [(0, 0)] * (first.ndim - 2) + [(3 - k, 0), (0, 0)])
        for k in range(1, 4)
    )


def tail_taps(tail, taps):
    return sum(
        jnp.pad(taps[k] * tail[..., k:, :], [(0, 0)] * (tail.ndim - 2) + [(0, k), (0, 0)])
        for k in range(3)
    )


def near_groups():
    count = lax.axis_size("ctx")
    return [list(range(g * NEAR, (g + 1) * NEAR)) for g in range(count // NEAR)]


def first_update(total_x, total_b, scale):
    scaled = scale * jax.nn.silu(total_x).astype(jnp.bfloat16).astype(jnp.float32)
    return jnp.einsum(
        "...tc,...tn->...cn",
        scaled.astype(jnp.bfloat16),
        jax.nn.silu(total_b).astype(jnp.bfloat16),
        preferred_element_type=jnp.float32,
    )


def entering_states(message, conv_x, conv_b):
    f32, bf16 = jnp.float32, jnp.bfloat16
    near = near_groups()
    place = lax.axis_index("ctx") % NEAR
    taps_x = lax.dynamic_slice_in_dim(conv_x, place * 128, 128, 1)
    taps_b = conv_b
    rest = message[:, 128:].astype(f32)
    part_decays = rest[:, 0:2] + rest[:, 2:4] + rest[:, 4:6]
    first_x, tail_x, first_b, tail_b = (rest[:, 6 + 3 * i : 9 + 3 * i] for i in range(4))
    scale = rest[:, 18:21] + rest[:, 21:24] + rest[:, 24:27]
    shifted = [jnp.pad(v[:-1], ((1, 0), (0, 0), (0, 0))) for v in (tail_x, tail_b)]
    parts = message[:, :128].astype(f32) + first_update(
        own_taps(first_x, taps_x) + tail_taps(shifted[0], taps_x),
        own_taps(first_b, taps_b) + tail_taps(shifted[1], taps_b),
        scale,
    )
    inside, decays = [jnp.zeros((128, 128), f32)], [jnp.ones((2, 128), f32)]
    after = [jnp.zeros((2, 128), f32), jnp.ones((2, 128), f32)]
    for k in range(NEAR):
        inside.append(widen(part_decays[k]) * inside[-1] + parts[k])
        decays.append(decays[-1] * part_decays[k])
        if k:
            after.append(after[-1] * part_decays[k])
    total, decay = inside[NEAR], widen(decays[NEAR])
    ends = message[NEAR - 1, 128 + 9 : 128 + 18]
    ends = jnp.pad(jnp.concatenate([ends[0:3], ends[6:9]], axis=0), ((0, 10), (0, 0)))
    own_x, own_b = own_taps(first_x[0], taps_x), own_taps(first_b[0], taps_b)
    without = first_update(own_x, own_b, scale[0])

    def change(rows):
        x_part, b_part = tail_taps(rows[0:3], taps_x), tail_taps(rows[3:6], taps_b)
        return first_update(own_x + x_part, own_b + b_part, scale[0])

    behind = widen(after[NEAR])
    total, base = total.astype(bf16), total - behind * without
    base, own_x, own_b, ends = lax.optimization_barrier((base, own_x, own_b, ends))
    before, rows = jnp.zeros((128, 128), f32), jnp.zeros((16, 128), f32)
    on = total
    for g in range(len(near) - 1):
        sent = jnp.concatenate([on, ends], axis=0)
        came = lax.ppermute(sent, "ctx", [(i, i + NEAR) for i in near[g]]).astype(f32)
        on = (decay * came[:128] + base + behind * change(came[128:])).astype(bf16)
        before, rows = before + came[:128], rows + came[128:]
    change = change(rows) - without
    inside = jnp.stack(inside[:NEAR]) + widen(jnp.stack(after[:NEAR])) * change
    inside = lax.optimization_barrier(inside)
    decays = lax.optimization_barrier(jnp.stack(decays[:NEAR]))
    states = (inside + widen(decays) * before).astype(bf16)
    states = lax.all_to_all(states, "ctx", 0, 0, tiled=True, axis_index_groups=near)
    return states.reshape(NEAR * 128, 128)


def halo(tails):
    count = lax.axis_size("ctx")
    return lax.ppermute(tails, "ctx", [(i, i + 1) for i in range(count - 1)])


def shards(
    x_in, z_in, b_in, c_in, dt_raw, dt_bias, a_log, d_skip, conv_x, conv_b, conv_c, norm_gain
):
    length, width = x_in.shape
    heads = dt_raw.shape[1]
    head_size = width // heads
    state = b_in.shape[1]
    count = lax.axis_size("ctx")
    whole = width + 2 * state
    f32, bf16 = jnp.float32, jnp.bfloat16
    shape = jax.ShapeDtypeStruct
    message, logs, delta = pl.pallas_call(
        without_halo,
        out_shape=[
            shape((width // 128, 128 + EXTRA, state), bf16),
            shape((heads, length), f32),
            shape((heads, length), f32),
        ],
        scratch_shapes=[
            pltpu.VMEM((8 + length, 128), f32),
            pltpu.VMEM((8 + length, 128), f32),
            pltpu.VMEM((EXTRA, 128), f32),
        ],
        compiler_params=pltpu.CompilerParams(vmem_limit_bytes=HIGH),
        name="without_halo",
    )(x_in, b_in, dt_raw.T, dt_bias[None], a_log[None], conv_x, conv_b)
    late_x, late_b, late_c, _ = lax.optimization_barrier((x_in, b_in, c_in, message))
    end = length // 16 - 1
    tails = pl.pallas_call(
        pack_tails,
        grid=(1,),
        in_specs=[pl.BlockSpec((16, v), lambda i: (end, 0)) for v in (width, state, state)],
        out_specs=pl.BlockSpec((16, whole), lambda i: (0, 0)),
        out_shape=shape((16, whole), bf16),
        name="pack_tails",
    )(late_x, late_b, late_c)
    tails = halo(tails)
    x_act, b_act, c_act = pl.pallas_call(
        all_rows,
        out_shape=[shape((length, v), bf16) for v in (width, state, state)],
        scratch_shapes=[pltpu.VMEM((8 + length, 128), f32)],
        compiler_params=pltpu.CompilerParams(vmem_limit_bytes=LOW),
        name="all_rows",
    )(tails, late_x, late_b, late_c, conv_x, conv_b, conv_c)
    message = lax.all_to_all(message, "ctx", 0, 0, tiled=True, axis_index_groups=near_groups())
    message, x_act, b_act, c_act = lax.optimization_barrier((message, x_act, b_act, c_act))
    lower = jnp.triu(jnp.ones((SPAN, SPAN), dtype=bool))
    x_heads = x_act.T.reshape(heads, head_size, length)
    scores = jnp.dot(b_act, c_act.T, preferred_element_type=f32)
    decay = jnp.exp(jnp.where(lower[None], logs[:, None, :] - logs[:, :, None], -jnp.inf))
    weights = (scores[None] * decay * delta[:, :, None]).astype(bf16)
    inner = jnp.einsum("hst,hps->hpt", weights, x_heads, preferred_element_type=f32)
    inner = inner + d_skip[:, None, None] * x_heads.astype(f32)
    gate = jax.nn.silu(z_in.astype(f32)).T
    gain = gate * norm_gain[:, None]
    inner, gate, gain, grown = lax.optimization_barrier((inner, gate, gain, jnp.exp(logs)))
    state_low = entering_states(message, conv_x, conv_b)
    outer = jnp.dot(state_low, c_act.T, preferred_element_type=f32)
    y_val = inner + grown[:, None, :] * outer.reshape(heads, head_size, length)
    y_val = y_val.reshape(width, length)
    gated = y_val * gate
    meansq = jnp.mean(gated * gated, axis=0, keepdims=True)
    normed = (y_val * gain * lax.rsqrt(meansq + 1e-05)).astype(bf16)
    return lax.all_to_all(normed, "ctx", split_axis=0, concat_axis=1, tiled=True)


def solution(mesh):
    return jax.shard_map(
        shards,
        mesh=mesh,
        in_specs=(
            P("ctx", "tp"),
            P("ctx", "tp"),
            P("ctx", "tp"),
            P("ctx", "tp"),
            P("ctx", "tp"),
            P("tp"),
            P("tp"),
            P("tp"),
            P(None, "tp"),
            P(None, "tp"),
            P(None, "tp"),
            P("tp"),
        ),
        out_specs=P(("tp", "ctx"), None),
        check_vma=False,
    )
```

time: 142 us -> 141 us (level)
  waiting for transfers between devices: 27.5 us -> 10.4 us
  starting transfers between devices: 20.3 us -> 32.8 us
  matrix products: 1.12 us -> 3.33 us
    all_to_all x1, starting transfers between devices: 3.48 us -> 17.5 us  [shards(): lax.all_to_all(message, 'ctx', 0, 0, tiled=True, axis_index_groups=near_g...]
    ppermute x8, waiting for transfers between devices: 12.4 us -> 1.59 us  [the longest x7 0.8 us: entering_states(): lax.ppermute(sent, 'ctx', [(i, i + NEAR) for i in near[g]]).astype(f32)]
    all_to_all x1, waiting for transfers between devices: 9.37 us -> 3.1 us  [shards(): lax.all_to_all(message, 'ctx', 0, 0, tiled=True, axis_index_groups=near_g...]
    ppermute x8, starting transfers between devices: 11.4 us -> 8.81 us  [the longest x7 5.27 us: entering_states(): lax.ppermute(sent, 'ctx', [(i, i + NEAR) for i in near[g]]).astype(f32)]
    dot_general x0 -> x9, matrix products: none -> 2.22 us  [first_update(): jnp.einsum('...tc,...tn->...cn', scaled.astype(jnp.bfloat16), jax.nn.silu...]
    pallas_call x1 -> x2, Pallas kernels: 2.07 us -> 3.36 us  [the longest x1 2.98 us: shards(): pl.pallas_call(without_halo, out_shape=[shape((width // 128, 128 + EXTRA,...]
  transfers between devices with their start and end apart: 10 -> 10, of which waited for: 4 -> 4; matrix products, arithmetic and copies ran while one was open for 1% -> 1% of each run, Pallas kernels for 0% -> 1%
where the time goes in v3:
time: 141 us; the launch traced here: 140 us
  blocking collectives  83 us (59%)
  starting transfers between devices  32.8 us (23%)
  waiting for transfers between devices  10.4 us (7%)
  Pallas kernels  4.82 us (3%)
  matrix products  3.33 us (2%)
  local copies, waits for them, and re-layouts  3.07 us (2%)
  other arithmetic  2.19 us (2%)
    all_to_all x1, blocking collectives, shards(): lax.all_to_all(normed, 'ctx', split_axis=0, concat_axis=1, tiled=True)  83 us
    all_to_all x1, starting transfers between devices, shards(): lax.all_to_all(message, 'ctx', 0, 0, tiled=True, axis_index_groups=near_g...  17.5 us
    all_to_all x1, starting transfers between devices, entering_states(): lax.all_to_all(states, 'ctx', 0, 0, tiled=True, axis_index_groups=near)  6.55 us
    all_to_all x1, waiting for transfers between devices, entering_states(): lax.all_to_all(states, 'ctx', 0, 0, tiled=True, axis_index_groups=near)  5.74 us
    ppermute x7, starting transfers between devices, entering_states(): lax.ppermute(sent, 'ctx', [(i, i + NEAR) for i in near[g]]).astype(f32)  5.27 us
    ppermute x1, starting transfers between devices, halo(): return lax.ppermute(tails, 'ctx', [(i, i + 1) for i in range(count - 1)])  3.53 us
    all_to_all x1, waiting for transfers between devices, shards(): lax.all_to_all(message, 'ctx', 0, 0, tiled=True, axis_index_groups=near_g...  3.1 us
    pallas_call x1, Pallas kernels, shards(): pl.pallas_call(without_halo, out_shape=[shape((width // 128, 128 + EXTRA,...  2.98 us
  transfers between devices with their start and end apart: 10, of which 4 were waited for; matrix products, arithmetic and copies ran while one was open for 1% of the time, Pallas kernels for 1%

profile of v3, /device:TPU:1, one launch (start us, length us, event | category | flops | bytes accessed | tf_op | source)
XLA Modules:
  0.0 140.5 jit_solution(11944748628461514413)
XLA Ops:
  0.0 3.0 %without_halo.1 = (bf16[8,160,128]{2,1,0:T(8,128)(2,1)}, f32[16,128]{1,0:T(8,128)}, f32[16,128]{1,0:T(8,128)}) custom-call(bf16[128,1024]{1,0:T(8,128)(2,1)} %x_ref.3, bf16[128,128]{1,0:T(8,128)(2,1)} %b_ref.3, f32[16,128]{1,0:T(8,128)} %bitcast.417, f32[1,16]{1,0:T(1,128)} %bitcast.418, f32[1,16]{1,0:T(1,128)} %bitcast.419, f32[4,1024]{1,0:T(4,128)} %tx_ref.3, ...), custom_call_target="tpu_custom_call" | custom-call | tf_op jit(solution)/shard_map/without_halo/pallas_call | solution.py:205
  3.0 17.5 %all-to-all-start = ((bf16[8,160,128]{2,1,0:T(8,128)(2,1)}), bf16[8,160,128]{2,1,0:T(8,128)(2,1)S(1)}, u32[]{:S(2)}, u32[]{:S(2)}) async-start(bf16[8,160,128]{2,1,0:T(8,128)(2,1)} %get-tuple-element.26), calls=%async_computation | async-start | bytes 655360 | tf_op jit(solution)/shard_map/all_to_all | solution.py:238
  20.5 1.5 %pack_tails.1 = bf16[16,1280]{1,0:T(8,128)(2,1)} custom-call(bf16[128,1024]{1,0:T(8,128)(2,1)} %x_ref.3, bf16[128,128]{1,0:T(8,128)(2,1)} %b_ref.3, bf16[128,128]{1,0:T(8,128)(2,1)} %c_ref.1), custom_call_target="tpu_custom_call" | custom-call | tf_op jit(solution)/shard_map/pack_tails/pallas_call | solution.py:222
  21.9 3.5 %collective-permute-start = (bf16[16,1280]{1,0:T(8,128)(2,1)}, bf16[16,1280]{1,0:T(8,128)(2,1)S(1)}, u32[]{:S(2)}, u32[]{:S(2)}) collective-permute-start(bf16[16,1280]{1,0:T(8,128)(2,1)} %pack_tails.1), channel_id=1, source_target_pairs={{0,16},{16,32},{32,48},{48,64},{64,80},{80,96},{96,112},{112,128},... | collective-permute-start | bytes 122888 | tf_op jit(solution)/shard_map/ppermute | solution.py:191
  25.5 0.0 copy-start.3
  25.5 0.0 copy-start.4
  25.5 0.0 copy-start.5
  25.5 0.7 copy-done.3
  26.2 0.8 collective-permute-done.tail_ref
  27.0 0.4 all_rows.1
  27.4 3.1 %all-to-all-done = bf16[8,160,128]{2,1,0:T(8,128)(2,1)S(1)} async-done(((bf16[8,160,128]{2,1,0:T(8,128)(2,1)}), bf16[8,160,128]{2,1,0:T(8,128)(2,1)S(1)}, u32[]{:S(2)}, u32[]{:S(2)}) %all-to-all-start) | async-done | bytes 327712 | tf_op jit(solution)/shard_map/all_to_all | solution.py:238
  30.8 0.3 convolution_add_fusion
  31.2 0.1 fusion.196
  31.2 0.2 fusion.36
  31.5 1.3 collective-permute-start.1
  33.0 0.8 collective-permute-done.1
  33.9 0.2 fusion.20
  34.1 0.7 collective-permute-start.2
  34.9 0.2 fusion.23
  35.2 0.7 collective-permute-start.3
  35.9 0.2 fusion.26
  36.2 0.7 collective-permute-start.4
  36.9 0.2 fusion.29
  37.2 0.7 collective-permute-start.5
  37.9 0.2 fusion.32
  38.2 0.7 collective-permute-start.6
  38.9 0.2 fusion.35
  39.2 0.7 collective-permute-start.7
  40.0 0.2 convolution_subtract_fusion
  40.2 0.8 fusion.10
  41.0 6.6 %all-to-all-start.1 = ((bf16[8,128,128]{2,1,0:T(8,128)(2,1)}), bf16[8,128,128]{2,1,0:T(8,128)(2,1)S(1)}, u32[]{:S(2)}, u32[]{:S(2)}) async-start(bf16[8,128,128]{2,1,0:T(8,128)(2,1)} %fusion.10), calls=%async_computation.1 | async-start | bytes 524288 | tf_op jit(solution)/shard_map/all_to_all | solution.py:185
  47.6 0.2 copy.21
  47.8 0.1 fusion.52
  47.9 0.0 copy-start.8
  47.9 0.1 fusion.4
  48.0 0.5 copy-done.8
  48.6 0.2 broadcast_multiply_fusion
  48.8 0.2 copy.20
  49.0 0.1 fusion.200
  49.1 0.6 copy-done.9
  49.7 0.1 copy-done.10
  49.8 0.8 convolution_add_fusion.1
  50.5 5.7 %all-to-all-done.1 = bf16[8,128,128]{2,1,0:T(8,128)(2,1)S(1)} async-done(((bf16[8,128,128]{2,1,0:T(8,128)(2,1)}), bf16[8,128,128]{2,1,0:T(8,128)(2,1)S(1)}, u32[]{:S(2)}, u32[]{:S(2)}) %all-to-all-start.1) | async-done | bytes 262176 | tf_op jit(solution)/shard_map/all_to_all | solution.py:185
  56.3 0.2 fusion
  56.5 0.2 fusion.8
  56.7 0.1 fusion.6
  56.8 83.0 %all_to_all.29 = bf16[64,16,128]{2,1,0:T(8,128)(2,1)S(1)} all-to-all(bf16[64,16,128]{2,1,0:T(8,128)(2,1)S(1)} %bitcast.405), channel_id=1, replica_groups=mesh['ctx'=64,'tp'=16] {'ctx'}, dimensions={0} | all-to-all | bytes 524288 | tf_op jit(solution)/shard_map/all_to_all | solution.py:257
  139.8 0.7 copy_bitcast_fusion
  (98 shorter events, 0.9 us)
Async XLA Ops:
  3.0 27.5 %all-to-all-start = ((bf16[8,160,128]{2,1,0:T(8,128)(2,1)}), bf16[8,160,128]{2,1,0:T(8,128)(2,1)S(1)}, u32[]{:S(2)}, u32[]{:S(2)}) async-start(bf16[8,160,128]{2,1,0:T(8,128)(2,1)} %get-tuple-element.26), calls=%async_computation | async-start | bytes 655360 | tf_op jit(solution)/shard_map/all_to_all | solution.py:238
  20.5 6.5 %copy-start = (bf16[128,1024]{1,0:T(8,128)(2,1)S(1)}, bf16[128,1024]{1,0:T(8,128)(2,1)}, u32[]{:S(2)}) copy-start(bf16[128,1024]{1,0:T(8,128)(2,1)} %x_ref.3) | copy-start | bytes 786436
  21.9 5.1 %collective-permute-start = (bf16[16,1280]{1,0:T(8,128)(2,1)}, bf16[16,1280]{1,0:T(8,128)(2,1)S(1)}, u32[]{:S(2)}, u32[]{:S(2)}) collective-permute-start(bf16[16,1280]{1,0:T(8,128)(2,1)} %pack_tails.1), channel_id=1, source_target_pairs={{0,16},{16,32},{32,48},{48,64},{64,80},{80,96},{96,112},{112,128},... | collective-permute-start | bytes 122888 | tf_op jit(solution)/shard_map/ppermute | solution.py:191
  25.5 0.7 copy-start.3
  25.5 1.5 %copy-start.4 = (f32[4,128]{1,0:T(4,128)S(1)}, f32[4,128]{1,0:T(4,128)}, u32[]{:S(2)}) copy-start(f32[4,128]{1,0:T(4,128)} %tb_ref.3) | copy-start | bytes 6148
  25.5 1.5 %copy-start.5 = (f32[4,128]{1,0:T(4,128)S(1)}, f32[4,128]{1,0:T(4,128)}, u32[]{:S(2)}) copy-start(f32[4,128]{1,0:T(4,128)} %tc_ref.1) | copy-start | bytes 6148
  26.2 0.8 copy-start.1
  26.2 0.8 copy-start.2
  31.5 2.3 %collective-permute-start.1 = (bf16[144,128]{1,0:T(8,128)(2,1)S(1)}, bf16[144,128]{1,0:T(8,128)(2,1)S(1)}, u32[]{:S(2)}, u32[]{:S(2)}) collective-permute-start(bf16[144,128]{1,0:T(8,128)(2,1)S(1)} %pad_maximum_fusion.6), channel_id=1, source_target_pairs={{0,128},{16,144},{32,160},{48,176},{64,192},{80,208},{96,224},{112... | collective-permute-start | bytes 110600 | tf_op jit(solution)/shard_map/ppermute | solution.py:177
  34.1 0.7 collective-permute-start.2
  35.2 0.7 collective-permute-start.3
  36.2 0.7 collective-permute-start.4
  37.2 0.7 collective-permute-start.5
  38.2 0.7 collective-permute-start.6
  39.2 0.7 collective-permute-start.7
  41.0 6.6 %copy-start.7 = (f32[16,128]{1,0:T(8,128)S(1)}, f32[16,128]{1,0:T(8,128)}, u32[]{:S(2)}) copy-start(f32[16,128]{1,0:T(8,128)} %get-tuple-element.36) | copy-start | bytes 24580
  41.0 6.6 %copy-start.6 = (bf16[128,1024]{1,0:T(8,128)(2,1)S(1)}, bf16[128,1024]{1,0:T(8,128)(2,1)}, u32[]{:S(2)}) copy-start(bf16[128,1024]{1,0:T(8,128)(2,1)} %param.13) | copy-start | bytes 786436
  41.0 15.3 %all-to-all-start.1 = ((bf16[8,128,128]{2,1,0:T(8,128)(2,1)}), bf16[8,128,128]{2,1,0:T(8,128)(2,1)S(1)}, u32[]{:S(2)}, u32[]{:S(2)}) async-start(bf16[8,128,128]{2,1,0:T(8,128)(2,1)} %fusion.10), calls=%async_computation.1 | async-start | bytes 524288 | tf_op jit(solution)/shard_map/all_to_all | solution.py:185
  47.9 0.7 copy-start.8
  49.0 0.7 copy-start.9
  49.1 0.7 copy-start.10

commit v4 on v3

--- a/solution.py
+++ b/solution.py
@@ -158,30 +158,77 @@
         if k:
             after.append(after[-1] * part_decays[k])
     total, decay = inside[NEAR], widen(decays[NEAR])
-    ends = message[NEAR - 1, 128 + 9 : 128 + 18]
-    ends = jnp.pad(jnp.concatenate([ends[0:3], ends[6:9]], axis=0), ((0, 10), (0, 0)))
-    own_x, own_b = own_taps(first_x[0], taps_x), own_taps(first_b[0], taps_b)
-    without = first_update(own_x, own_b, scale[0])
-
-    def change(rows):
+    block = message[NEAR - 1, 128 + 9 : 128 + 18]
+    ends = jnp.pad(jnp.concatenate([block[0:3], block[6:9]], axis=0), ((0, 10), (0, 0)))
+    known = (own_taps(first_x[0], taps_x), own_taps(first_b[0], taps_b), scale[0])
+    without = first_update(*known)
+
+    def change(rows, own_x, own_b, scale):
         x_part, b_part = tail_taps(rows[0:3], taps_x), tail_taps(rows[3:6], taps_b)
-        return first_update(own_x + x_part, own_b + b_part, scale[0])
+        return first_update(own_x + x_part, own_b + b_part, scale)
+
+    def send(value, pairs):
+        pairs = [(i, i + NEAR * (t - g)) for g, t in pairs for i in near[g]]
+        return lax.ppermute(value, "ctx", pairs)
 
     behind = widen(after[NEAR])
-    total, base = total.astype(bf16), total - behind * without
-    base, own_x, own_b, ends = lax.optimization_barrier((base, own_x, own_b, ends))
-    before, rows = jnp.zeros((128, 128), f32), jnp.zeros((16, 128), f32)
-    on = total
-    for g in range(len(near) - 1):
+    base = total - behind * without
+    came = send(jnp.concatenate([total.astype(bf16), ends], axis=0), [(0, 1)]).astype(f32)
+    entry, rows = came[:128], came[128:]
+    base, known, ends = lax.optimization_barrier((base, known, ends))
+    half = len(near) // 2
+    for g in range(1, half):
+        on = (decay * came[:128] + base + behind * change(came[128:], *known)).astype(bf16)
         sent = jnp.concatenate([on, ends], axis=0)
-        came = lax.ppermute(sent, "ctx", [(i, i + NEAR) for i in near[g]]).astype(f32)
-        on = (decay * came[:128] + base + behind * change(came[128:])).astype(bf16)
-        before, rows = before + came[:128], rows + came[128:]
-    change = change(rows) - without
-    inside = jnp.stack(inside[:NEAR]) + widen(jnp.stack(after[:NEAR])) * change
-    inside = lax.optimization_barrier(inside)
-    decays = lax.optimization_barrier(jnp.stack(decays[:NEAR]))
-    states = (inside + widen(decays) * before).astype(bf16)
+        if g < half - 1:
+            came = send(sent, [(g, g + 1)])
+            if g == 1:
+                base_low, came = lax.optimization_barrier((base.astype(bf16), came))
+            came = came.astype(f32)
+            entry, rows = entry + came[:128], rows + came[128:]
+    thirds = [
+        lax.reduce_precision(v, 8, 7)
+        for d in (decays[NEAR], after[NEAR])
+        for v in (d, d - lax.reduce_precision(d, 8, 7))
+    ]
+    extra = [first_x[0], first_b[0], *(rest[0, 18 + 3 * i : 21 + 3 * i] for i in range(3)), *thirds]
+    extra = jnp.concatenate(extra, axis=0).astype(bf16)
+    extra = jnp.pad(extra, ((0, 32 - extra.shape[0]), (0, 0)))
+    even = jnp.concatenate([base_low, ends, extra], axis=0)
+    groups = len(near)
+    even = send(even, [(g, g + 1) for g in range(half, groups, 2)])
+    far = jnp.zeros((144, 128), f32)
+    for g in range(half - 1, groups - 1, 2):
+        sent = jnp.concatenate([on, ends], axis=0)
+        came = send(sent, [(g, g + 2)])
+        if g == groups - 3:
+            sent, came = lax.optimization_barrier((sent, came))
+        if g == half - 1:
+            even, came = lax.optimization_barrier((even, came))
+            even = even.astype(f32)
+            base_e, ends_e, extra = even[:128], even[128:144], even[144:]
+            known_e = (
+                own_taps(extra[0:3], taps_x),
+                own_taps(extra[3:6], taps_b),
+                extra[6:9] + extra[9:12] + extra[12:15],
+            )
+            decay_e = widen(extra[15:17] + extra[17:19])
+            behind_e = widen(extra[19:21] + extra[21:23])
+            rows = rows + ends_e
+            odd = (decay * decay_e, decay * base_e + base + behind * change(ends_e, *known))
+            odd = lax.optimization_barrier((*odd, decay * behind_e, decay_e, base_e, behind_e, known_e))
+            step, own, first_e, decay_e, base_e, behind_e, known_e = odd
+        came = came.astype(f32)
+        beside = send(sent, [(g, g + 1)]).astype(f32)
+        entry, rows, far = entry + beside[:128], rows + beside[128:], far + came
+        on = (step * came[:128] + own + first_e * change(came[128:], *known_e)).astype(bf16)
+    inside = jnp.stack(inside[:NEAR]) + widen(jnp.stack(after[:NEAR])) * (
+        change(rows, *known) - without
+    )
+    decays = widen(jnp.stack(decays[:NEAR]))
+    inside, decays, entry = lax.optimization_barrier((inside, decays, entry + base_e))
+    before = entry + decay_e * far[:128] + behind_e * change(far[128:], *known_e)
+    states = (inside + decays * before).astype(bf16)
     states = lax.all_to_all(states, "ctx", 0, 0, tiled=True, axis_index_groups=near)
     return states.reshape(NEAR * 128, 128)
 

time: 141 us -> 137 us (0.972)
  blocking collectives: 83 us -> 77.5 us
    all_to_all x1, blocking collectives: 83 us -> 77.5 us  [shards(): lax.all_to_all(normed, 'ctx', split_axis=0, concat_axis=1, tiled=True)]
    ppermute x7 -> x8, starting transfers between devices: 5.27 us -> 5.94 us  [send(): return lax.ppermute(value, 'ctx', pairs)]
  transfers between devices with their start and end apart: 10 -> 11, of which waited for: 4 -> 4; matrix products, arithmetic and copies ran while one was open for 1% -> 2% of each run, Pallas kernels for 1% -> 1%
where the time goes in v4:
time: 137 us; the launch traced here: 136 us
  blocking collectives  77.5 us (57%)
  starting transfers between devices  33.5 us (24%)
  waiting for transfers between devices  10.3 us (8%)
  Pallas kernels  4.82 us (4%)
  local copies, waits for them, and re-layouts  3.4 us (2%)
  matrix products  3.34 us (2%)
  other arithmetic  2.22 us (2%)
    all_to_all x1, blocking collectives, shards(): lax.all_to_all(normed, 'ctx', split_axis=0, concat_axis=1, tiled=True)  77.5 us
    all_to_all x1, starting transfers between devices, shards(): lax.all_to_all(message, 'ctx', 0, 0, tiled=True, axis_index_groups=near_g...  17.5 us
    all_to_all x1, starting transfers between devices, entering_states(): lax.all_to_all(states, 'ctx', 0, 0, tiled=True, axis_index_groups=near)  6.54 us
    ppermute x8, starting transfers between devices, send(): return lax.ppermute(value, 'ctx', pairs)  5.94 us
    all_to_all x1, waiting for transfers between devices, entering_states(): lax.all_to_all(states, 'ctx', 0, 0, tiled=True, axis_index_groups=near)  5.74 us
    ppermute x1, starting transfers between devices, halo(): return lax.ppermute(tails, 'ctx', [(i, i + 1) for i in range(count - 1)])  3.53 us
    all_to_all x1, waiting for transfers between devices, shards(): lax.all_to_all(message, 'ctx', 0, 0, tiled=True, axis_index_groups=near_g...  3.11 us
    pallas_call x1, Pallas kernels, shards(): pl.pallas_call(without_halo, out_shape=[shape((width // 128, 128 + EXTRA,...  2.99 us
  transfers between devices with their start and end apart: 11, of which 4 were waited for; matrix products, arithmetic and copies ran while one was open for 2% of the time, Pallas kernels for 1%

profile of v4, /device:TPU:1, one launch (start us, length us, event | category | flops | bytes accessed | tf_op | source)
XLA Modules:
  0.0 135.9 jit_solution(9478855155478082780)
XLA Ops:
  0.0 3.0 %without_halo.1 = (bf16[8,160,128]{2,1,0:T(8,128)(2,1)}, f32[16,128]{1,0:T(8,128)}, f32[16,128]{1,0:T(8,128)}) custom-call(bf16[128,1024]{1,0:T(8,128)(2,1)} %x_ref.3, bf16[128,128]{1,0:T(8,128)(2,1)} %b_ref.3, f32[16,128]{1,0:T(8,128)} %bitcast.385, f32[1,16]{1,0:T(1,128)} %bitcast.386, f32[1,16]{1,0:T(1,128)} %bitcast.387, f32[4,1024]{1,0:T(4,128)} %tx_ref.3, ...), custom_call_target="tpu_custom_call" | custom-call | tf_op jit(solution)/shard_map/without_halo/pallas_call | solution.py:252
  3.0 17.5 %all-to-all-start = ((bf16[8,160,128]{2,1,0:T(8,128)(2,1)}), bf16[8,160,128]{2,1,0:T(8,128)(2,1)S(1)}, u32[]{:S(2)}, u32[]{:S(2)}) async-start(bf16[8,160,128]{2,1,0:T(8,128)(2,1)} %get-tuple-element.45), calls=%async_computation | async-start | bytes 655360 | tf_op jit(solution)/shard_map/all_to_all | solution.py:285
  20.5 1.5 %pack_tails.1 = bf16[16,1280]{1,0:T(8,128)(2,1)} custom-call(bf16[128,1024]{1,0:T(8,128)(2,1)} %x_ref.3, bf16[128,128]{1,0:T(8,128)(2,1)} %b_ref.3, bf16[128,128]{1,0:T(8,128)(2,1)} %c_ref.1), custom_call_target="tpu_custom_call" | custom-call | tf_op jit(solution)/shard_map/pack_tails/pallas_call | solution.py:269
  21.9 3.5 %collective-permute-start = (bf16[16,1280]{1,0:T(8,128)(2,1)}, bf16[16,1280]{1,0:T(8,128)(2,1)S(1)}, u32[]{:S(2)}, u32[]{:S(2)}) collective-permute-start(bf16[16,1280]{1,0:T(8,128)(2,1)} %pack_tails.1), channel_id=1, source_target_pairs={{0,16},{16,32},{32,48},{48,64},{64,80},{80,96},{96,112},{112,128},... | collective-permute-start | bytes 122888 | tf_op jit(solution)/shard_map/ppermute | solution.py:238
  25.5 0.0 copy-start.3
  25.5 0.0 copy-start.4
  25.5 0.7 copy-done.3
  26.2 0.0 copy-start.5
  26.3 0.7 collective-permute-done.tail_ref
  27.0 0.4 all_rows.1
  27.4 3.1 %all-to-all-done = bf16[8,160,128]{2,1,0:T(8,128)(2,1)S(1)} async-done(((bf16[8,160,128]{2,1,0:T(8,128)(2,1)}), bf16[8,160,128]{2,1,0:T(8,128)(2,1)S(1)}, u32[]{:S(2)}, u32[]{:S(2)}) %all-to-all-start) | async-done | bytes 327712 | tf_op jit(solution)/shard_map/all_to_all | solution.py:285
  30.8 0.3 convolution_add_fusion
  31.2 1.3 collective-permute-start.1
  32.9 0.7 collective-permute-done.1
  33.6 0.2 fusion.23
  33.9 0.2 fusion.26
  34.1 0.7 collective-permute-start.2
  34.8 0.2 concatenate.29
  35.1 0.2 fusion.5
  35.4 0.7 collective-permute-start.3
  36.1 0.7 collective-permute-start.4
  36.8 0.2 fusion.30
  37.1 0.7 collective-permute-start.5
  37.7 0.7 collective-permute-start.6
  38.6 0.2 fusion.3
  38.8 0.2 fusion.6
  39.1 0.7 collective-permute-start.7
  39.8 0.7 collective-permute-start.8
  40.6 0.2 convolution_subtract_fusion
  41.0 0.2 fusion.1
  41.2 0.8 add_convert_fusion
  42.0 6.5 %all-to-all-start.1 = ((bf16[8,128,128]{2,1,0:T(8,128)(2,1)}), bf16[8,128,128]{2,1,0:T(8,128)(2,1)S(1)}, u32[]{:S(2)}, u32[]{:S(2)}) async-start(bf16[8,128,128]{2,1,0:T(8,128)(2,1)} %add_convert_fusion), calls=%async_computation.1 | async-start | bytes 524288 | tf_op jit(solution)/shard_map/all_to_all | solution.py:232
  48.6 0.2 copy.21
  48.7 0.1 fusion.50
  48.8 0.1 fusion.10
  49.0 0.5 copy-done.8
  49.5 0.2 broadcast_multiply_fusion
  49.7 0.2 copy.20
  49.9 0.1 fusion.204
  50.1 0.6 copy-done.9
  50.6 0.1 copy-done.10
  50.8 0.8 convolution_add_fusion.1
  51.5 5.7 %all-to-all-done.1 = bf16[8,128,128]{2,1,0:T(8,128)(2,1)S(1)} async-done(((bf16[8,128,128]{2,1,0:T(8,128)(2,1)}), bf16[8,128,128]{2,1,0:T(8,128)(2,1)S(1)}, u32[]{:S(2)}, u32[]{:S(2)}) %all-to-all-start.1) | async-done | bytes 262176 | tf_op jit(solution)/shard_map/all_to_all | solution.py:232
  57.3 0.2 fusion
  57.5 0.2 fusion.14
  57.7 0.1 fusion.12
  57.7 77.5 %all_to_all.29 = bf16[64,16,128]{2,1,0:T(8,128)(2,1)S(1)} all-to-all(bf16[64,16,128]{2,1,0:T(8,128)(2,1)S(1)} %bitcast.371), channel_id=1, replica_groups=mesh['ctx'=64,'tp'=16] {'ctx'}, dimensions={0} | all-to-all | bytes 524288 | tf_op jit(solution)/shard_map/all_to_all | solution.py:304
  135.2 0.7 copy_bitcast_fusion
  (107 shorter events, 1.0 us)
Async XLA Ops:
  3.0 27.5 %all-to-all-start = ((bf16[8,160,128]{2,1,0:T(8,128)(2,1)}), bf16[8,160,128]{2,1,0:T(8,128)(2,1)S(1)}, u32[]{:S(2)}, u32[]{:S(2)}) async-start(bf16[8,160,128]{2,1,0:T(8,128)(2,1)} %get-tuple-element.45), calls=%async_computation | async-start | bytes 655360 | tf_op jit(solution)/shard_map/all_to_all | solution.py:285
  20.5 6.5 %copy-start = (bf16[128,1024]{1,0:T(8,128)(2,1)S(1)}, bf16[128,1024]{1,0:T(8,128)(2,1)}, u32[]{:S(2)}) copy-start(bf16[128,1024]{1,0:T(8,128)(2,1)} %x_ref.3) | copy-start | bytes 786436
  21.9 5.1 %collective-permute-start = (bf16[16,1280]{1,0:T(8,128)(2,1)}, bf16[16,1280]{1,0:T(8,128)(2,1)S(1)}, u32[]{:S(2)}, u32[]{:S(2)}) collective-permute-start(bf16[16,1280]{1,0:T(8,128)(2,1)} %pack_tails.1), channel_id=1, source_target_pairs={{0,16},{16,32},{32,48},{48,64},{64,80},{80,96},{96,112},{112,128},... | collective-permute-start | bytes 122888 | tf_op jit(solution)/shard_map/ppermute | solution.py:238
  25.5 0.7 copy-start.3
  25.5 0.7 copy-start.4
  26.2 0.8 copy-start.1
  26.2 0.8 copy-start.2
  26.2 0.8 copy-start.5
  31.2 2.3 %collective-permute-start.1 = (bf16[144,128]{1,0:T(8,128)(2,1)S(1)}, bf16[144,128]{1,0:T(8,128)(2,1)S(1)}, u32[]{:S(2)}, u32[]{:S(2)}) collective-permute-start(bf16[144,128]{1,0:T(8,128)(2,1)S(1)} %pad_maximum_fusion.4), channel_id=1, source_target_pairs={{0,128},{16,144},{32,160},{48,176},{64,192},{80,208},{96,224},{112... | collective-permute-start | bytes 110600 | tf_op jit(solution)/shard_map/ppermute | solution.py:172
  34.1 0.9 collective-permute-start.2
  35.4 1.4 %collective-permute-start.3 = (bf16[144,128]{1,0:T(8,128)(2,1)S(1)}, bf16[144,128]{1,0:T(8,128)(2,1)S(1)}, u32[]{:S(2)}, u32[]{:S(2)}) collective-permute-start(bf16[144,128]{1,0:T(8,128)(2,1)S(1)} %pad_maximum_fusion.2), channel_id=1, source_target_pairs={{256,384},{272,400},{288,416},{304,432},{320,448},{336,464},{352,4... | collective-permute-start | bytes 110600 | tf_op jit(solution)/shard_map/ppermute | solution.py:172
  36.1 2.3 %collective-permute-start.4 = (bf16[176,128]{1,0:T(8,128)(2,1)S(1)}, bf16[176,128]{1,0:T(8,128)(2,1)S(1)}, u32[]{:S(2)}, u32[]{:S(2)}) collective-permute-start(bf16[176,128]{1,0:T(8,128)(2,1)S(1)} %fusion.52), channel_id=1, source_target_pairs={{512,640},{528,656},{544,672},{560,688},{576,704},{592,720},{608,7... | collective-permute-start | bytes 135176 | tf_op jit(solution)/shard_map/ppermute | solution.py:172
  37.1 1.4 %collective-permute-start.5 = (bf16[144,128]{1,0:T(8,128)(2,1)S(1)}, bf16[144,128]{1,0:T(8,128)(2,1)S(1)}, u32[]{:S(2)}, u32[]{:S(2)}) collective-permute-start(bf16[144,128]{1,0:T(8,128)(2,1)S(1)} %pad_maximum_fusion.1), channel_id=1, source_target_pairs={{384,640},{400,656},{416,672},{432,688},{448,704},{464,720},{480,7... | collective-permute-start | bytes 110600 | tf_op jit(solution)/shard_map/ppermute | solution.py:172
  37.7 2.0 %collective-permute-start.6 = (bf16[144,128]{1,0:T(8,128)(2,1)S(1)}, bf16[144,128]{1,0:T(8,128)(2,1)S(1)}, u32[]{:S(2)}, u32[]{:S(2)}) collective-permute-start(bf16[144,128]{1,0:T(8,128)(2,1)S(1)} %pad_maximum_fusion.1), channel_id=1, source_target_pairs={{384,512},{400,528},{416,544},{432,560},{448,576},{464,592},{480,6... | collective-permute-start | bytes 110600 | tf_op jit(solution)/shard_map/ppermute | solution.py:172
  39.1 0.7 collective-permute-start.7
  39.8 0.7 collective-permute-start.8
  42.0 6.5 %copy-start.7 = (f32[16,128]{1,0:T(8,128)S(1)}, f32[16,128]{1,0:T(8,128)}, u32[]{:S(2)}) copy-start(f32[16,128]{1,0:T(8,128)} %get-tuple-element.55) | copy-start | bytes 24580
  42.0 6.6 %copy-start.6 = (bf16[128,1024]{1,0:T(8,128)(2,1)S(1)}, bf16[128,1024]{1,0:T(8,128)(2,1)}, u32[]{:S(2)}) copy-start(bf16[128,1024]{1,0:T(8,128)(2,1)} %param.13) | copy-start | bytes 786436
  42.0 15.3 %all-to-all-start.1 = ((bf16[8,128,128]{2,1,0:T(8,128)(2,1)}), bf16[8,128,128]{2,1,0:T(8,128)(2,1)S(1)}, u32[]{:S(2)}, u32[]{:S(2)}) async-start(bf16[8,128,128]{2,1,0:T(8,128)(2,1)} %add_convert_fusion), calls=%async_computation.1 | async-start | bytes 524288 | tf_op jit(solution)/shard_map/all_to_all | solution.py:232
  48.8 0.7 copy-start.8
  49.9 0.7 copy-start.9
  50.1 0.7 copy-start.10

commit v5 on v4

--- a/solution.py
+++ b/solution.py
@@ -134,7 +134,7 @@
     )
 
 
-def entering_states(message, conv_x, conv_b):
+def entering_states(message, conv_x, conv_b, late, make_local):
     f32, bf16 = jnp.float32, jnp.bfloat16
     near = near_groups()
     place = lax.axis_index("ctx") % NEAR
@@ -183,7 +183,8 @@
         if g < half - 1:
             came = send(sent, [(g, g + 1)])
             if g == 1:
-                base_low, came = lax.optimization_barrier((base.astype(bf16), came))
+                base_low, late, came = lax.optimization_barrier((base.astype(bf16), late, came))
+                local = make_local(late)
             came = came.astype(f32)
             entry, rows = entry + came[:128], rows + came[128:]
     thirds = [
@@ -204,7 +205,7 @@
         if g == groups - 3:
             sent, came = lax.optimization_barrier((sent, came))
         if g == half - 1:
-            even, came = lax.optimization_barrier((even, came))
+            even, came, local = lax.optimization_barrier((even, came, local))
             even = even.astype(f32)
             base_e, ends_e, extra = even[:128], even[128:144], even[144:]
             known_e = (
@@ -230,7 +231,7 @@
     before = entry + decay_e * far[:128] + behind_e * change(far[128:], *known_e)
     states = (inside + decays * before).astype(bf16)
     states = lax.all_to_all(states, "ctx", 0, 0, tiled=True, axis_index_groups=near)
-    return states.reshape(NEAR * 128, 128)
+    return states.reshape(NEAR * 128, 128), local
 
 
 def halo(tails):
@@ -284,17 +285,19 @@
     )(tails, late_x, late_b, late_c, conv_x, conv_b, conv_c)
     message = lax.all_to_all(message, "ctx", 0, 0, tiled=True, axis_index_groups=near_groups())
     message, x_act, b_act, c_act = lax.optimization_barrier((message, x_act, b_act, c_act))
-    lower = jnp.triu(jnp.ones((SPAN, SPAN), dtype=bool))
-    x_heads = x_act.T.reshape(heads, head_size, length)
-    scores = jnp.dot(b_act, c_act.T, preferred_element_type=f32)
-    decay = jnp.exp(jnp.where(lower[None], logs[:, None, :] - logs[:, :, None], -jnp.inf))
-    weights = (scores[None] * decay * delta[:, :, None]).astype(bf16)
-    inner = jnp.einsum("hst,hps->hpt", weights, x_heads, preferred_element_type=f32)
-    inner = inner + d_skip[:, None, None] * x_heads.astype(f32)
-    gate = jax.nn.silu(z_in.astype(f32)).T
-    gain = gate * norm_gain[:, None]
-    inner, gate, gain, grown = lax.optimization_barrier((inner, gate, gain, jnp.exp(logs)))
-    state_low = entering_states(message, conv_x, conv_b)
+    def make_local(delta):
+        lower = jnp.triu(jnp.ones((SPAN, SPAN), dtype=bool))
+        x_heads = x_act.T.reshape(heads, head_size, length)
+        scores = jnp.dot(b_act, c_act.T, preferred_element_type=f32)
+        decay = jnp.exp(jnp.where(lower[None], logs[:, None, :] - logs[:, :, None], -jnp.inf))
+        weights = (scores[None] * decay * delta[:, :, None]).astype(bf16)
+        inner = jnp.einsum("hst,hps->hpt", weights, x_heads, preferred_element_type=f32)
+        inner = inner + d_skip[:, None, None] * x_heads.astype(f32)
+        gate = jax.nn.silu(z_in.astype(f32)).T
+        return inner, gate, gate * norm_gain[:, None], jnp.exp(logs)
+
+    state_low, local = entering_states(message, conv_x, conv_b, delta, make_local)
+    inner, gate, gain, grown = local
     outer = jnp.dot(state_low, c_act.T, preferred_element_type=f32)
     y_val = inner + grown[:, None, :] * outer.reshape(heads, head_size, length)
     y_val = y_val.reshape(width, length)

time: 137 us -> 136 us (level)
  blocking collectives: 77.5 us -> 92.1 us
  waiting for transfers between devices: 10.3 us -> 1.6 us
  starting transfers between devices: 33.5 us -> 27 us
    all_to_all x0 -> x1, blocking collectives: none -> 14.6 us  [entering_states(): lax.all_to_all(states, 'ctx', 0, 0, tiled=True, axis_index_groups=near)]
    all_to_all x1 -> x0, starting transfers between devices: 6.54 us -> none  [entering_states(): lax.all_to_all(states, 'ctx', 0, 0, tiled=True, axis_index_groups=near)]
    all_to_all x1 -> x0, waiting for transfers between devices: 5.74 us -> none  [entering_states(): lax.all_to_all(states, 'ctx', 0, 0, tiled=True, axis_index_groups=near)]
    all_to_all x1, waiting for transfers between devices: 3.11 us -> 1.04 us  [shards(): lax.all_to_all(message, 'ctx', 0, 0, tiled=True, axis_index_groups=near_g...]
  transfers between devices with their start and end apart: 11 -> 10, of which waited for: 4 -> 2; matrix products, arithmetic and copies ran while one was open for 2% -> 2% of each run, Pallas kernels for 1% -> 1%
where the time goes in v5:
time: 136 us
  blocking collectives  92.1 us (68%)
  starting transfers between devices  27 us (20%)
  Pallas kernels  4.8 us (4%)
  local copies, waits for them, and re-layouts  4.38 us (3%)
  matrix products  3.32 us (2%)
  other arithmetic  1.61 us (1%)
  waiting for transfers between devices  1.6 us (1%)
    all_to_all x1, blocking collectives, shards(): lax.all_to_all(normed, 'ctx', split_axis=0, concat_axis=1, tiled=True)  77.6 us
    all_to_all x1, starting transfers between devices, shards(): lax.all_to_all(message, 'ctx', 0, 0, tiled=True, axis_index_groups=near_g...  17.5 us
    all_to_all x1, blocking collectives, entering_states(): lax.all_to_all(states, 'ctx', 0, 0, tiled=True, axis_index_groups=near)  14.6 us
    ppermute x8, starting transfers between devices, send(): return lax.ppermute(value, 'ctx', pairs)  5.94 us
    ppermute x1, starting transfers between devices, halo(): return lax.ppermute(tails, 'ctx', [(i, i + 1) for i in range(count - 1)])  3.53 us
    unnamed x27, local copies, waits for them, and re-layouts  3.08 us
    pallas_call x1, Pallas kernels, shards(): pl.pallas_call(without_halo, out_shape=[shape((width // 128, 128 + EXTRA,...  2.98 us
  transfers between devices with their start and end apart: 10, of which 2 were waited for; matrix products, arithmetic and copies ran while one was open for 2% of the time, Pallas kernels for 1%

profile of v5, /device:TPU:1, one launch (start us, length us, event | category | flops | bytes accessed | tf_op | source)
XLA Modules:
  0.0 135.6 jit_solution(12804711444072824131)
XLA Ops:
  0.0 3.0 %without_halo.1 = (bf16[8,160,128]{2,1,0:T(8,128)(2,1)}, f32[16,128]{1,0:T(8,128)}, f32[16,128]{1,0:T(8,128)}) custom-call(bf16[128,1024]{1,0:T(8,128)(2,1)} %x_ref.3, bf16[128,128]{1,0:T(8,128)(2,1)} %b_ref.3, f32[16,128]{1,0:T(8,128)} %bitcast.385, f32[1,16]{1,0:T(1,128)} %bitcast.386, f32[1,16]{1,0:T(1,128)} %bitcast.387, f32[4,1024]{1,0:T(4,128)} %tx_ref.3, ...), custom_call_target="tpu_custom_call" | custom-call | tf_op jit(solution)/shard_map/without_halo/pallas_call | solution.py:253
  3.0 17.5 %all-to-all-start = ((bf16[8,160,128]{2,1,0:T(8,128)(2,1)}), bf16[8,160,128]{2,1,0:T(8,128)(2,1)S(1)}, u32[]{:S(2)}, u32[]{:S(2)}) async-start(bf16[8,160,128]{2,1,0:T(8,128)(2,1)} %get-tuple-element.46), calls=%async_computation | async-start | bytes 655360 | tf_op jit(solution)/shard_map/all_to_all | solution.py:286
  20.5 1.4 %pack_tails.1 = bf16[16,1280]{1,0:T(8,128)(2,1)} custom-call(bf16[128,1024]{1,0:T(8,128)(2,1)} %x_ref.3, bf16[128,128]{1,0:T(8,128)(2,1)} %b_ref.3, bf16[128,128]{1,0:T(8,128)(2,1)} %c_ref.1), custom_call_target="tpu_custom_call" | custom-call | tf_op jit(solution)/shard_map/pack_tails/pallas_call | solution.py:270
  21.9 3.5 %collective-permute-start = (bf16[16,1280]{1,0:T(8,128)(2,1)}, bf16[16,1280]{1,0:T(8,128)(2,1)S(1)}, u32[]{:S(2)}, u32[]{:S(2)}) collective-permute-start(bf16[16,1280]{1,0:T(8,128)(2,1)} %pack_tails.1), channel_id=1, source_target_pairs={{0,16},{16,32},{32,48},{48,64},{64,80},{80,96},{96,112},{112,128},... | collective-permute-start | bytes 122888 | tf_op jit(solution)/shard_map/ppermute | solution.py:239
  25.5 0.2 copy.21
  25.7 0.5 copy-done.3
  26.2 0.7 copy-done.4
  26.9 0.1 fusion.49
  27.0 0.0 copy-start.8
  27.0 0.1 fusion.9
  27.2 0.5 copy-done.8
  27.7 0.2 broadcast_multiply_fusion
  27.9 0.5 copy-done.7
  28.4 0.3 copy-done
  28.6 0.4 copy-done.5
  29.1 0.4 all_rows.1
  29.5 1.0 all-to-all-done
  30.8 0.3 convolution_add_fusion
  31.2 0.1 fusion.200
  31.2 1.3 collective-permute-start.1
  32.6 0.1 fusion.204
  33.0 0.5 collective-permute-done.1
  33.6 0.2 fusion.22
  33.9 0.2 fusion.25
  34.1 0.7 collective-permute-start.2
  34.8 0.2 copy.20
  35.0 0.2 concatenate.28
  35.3 0.2 fusion.4
  35.6 0.7 collective-permute-start.4
  36.2 0.7 collective-permute-start.3
  37.0 0.2 fusion.29
  37.2 0.7 collective-permute-start.5
  37.9 0.8 convolution_add_fusion.1
  38.7 0.7 collective-permute-start.6
  39.5 0.2 fusion.2
  39.8 0.2 fusion.5
  40.1 0.7 collective-permute-start.7
  40.8 0.7 collective-permute-start.8
  41.6 0.2 convolution_subtract_fusion
  41.9 0.2 fusion
  42.2 0.1 add_convert_fusion
  42.3 14.6 %all_to_all.29 = bf16[8,128,128]{2,1,0:T(8,128)(2,1)S(1)} all-to-all(bf16[8,128,128]{2,1,0:T(8,128)(2,1)S(1)} %add_convert_fusion), channel_id=1, replica_groups={{0,16,32,48,64,80,96,112},{128,144,160,176,192,208,224,240},{256,272,28..., dimensions={0} | all-to-all | bytes 524288 | tf_op jit(solution)/shard_map/all_to_all | solution.py:233
  56.8 0.2 fusion.52
  57.0 0.1 multiply_add_fusion
  57.1 0.2 fusion.13
  57.3 0.1 fusion.11
  57.3 77.6 %all_to_all.30 = bf16[64,16,128]{2,1,0:T(8,128)(2,1)S(1)} all-to-all(bf16[64,16,128]{2,1,0:T(8,128)(2,1)S(1)} %bitcast.371), channel_id=1, replica_groups=mesh['ctx'=64,'tp'=16] {'ctx'}, dimensions={0} | all-to-all | bytes 524288 | tf_op jit(solution)/shard_map/all_to_all | solution.py:307
  134.9 0.7 copy_bitcast_fusion
  (107 shorter events, 1.0 us)
Async XLA Ops:
  3.0 27.5 %all-to-all-start = ((bf16[8,160,128]{2,1,0:T(8,128)(2,1)}), bf16[8,160,128]{2,1,0:T(8,128)(2,1)S(1)}, u32[]{:S(2)}, u32[]{:S(2)}) async-start(bf16[8,160,128]{2,1,0:T(8,128)(2,1)} %get-tuple-element.46), calls=%async_computation | async-start | bytes 655360 | tf_op jit(solution)/shard_map/all_to_all | solution.py:286
  20.5 5.0 %copy-start.6 = (bf16[128,1024]{1,0:T(8,128)(2,1)S(1)}, bf16[128,1024]{1,0:T(8,128)(2,1)}, u32[]{:S(2)}) copy-start(bf16[128,1024]{1,0:T(8,128)(2,1)} %param.13) | copy-start | bytes 786436
  21.9 6.5 %collective-permute-start = (bf16[16,1280]{1,0:T(8,128)(2,1)}, bf16[16,1280]{1,0:T(8,128)(2,1)S(1)}, u32[]{:S(2)}, u32[]{:S(2)}) collective-permute-start(bf16[16,1280]{1,0:T(8,128)(2,1)} %pack_tails.1), channel_id=1, source_target_pairs={{0,16},{16,32},{32,48},{48,64},{64,80},{80,96},{96,112},{112,128},... | collective-permute-start | bytes 122888 | tf_op jit(solution)/shard_map/ppermute | solution.py:239
  25.5 0.7 copy-start.3
  26.2 0.7 copy-start.4
  27.0 0.7 copy-start.8
  27.7 0.7 copy-start.7
  27.7 1.0 copy-start
  27.7 1.0 copy-start.1
  27.7 1.0 copy-start.2
  28.4 0.7 copy-start.5
  31.2 2.3 %collective-permute-start.1 = (bf16[144,128]{1,0:T(8,128)(2,1)S(1)}, bf16[144,128]{1,0:T(8,128)(2,1)S(1)}, u32[]{:S(2)}, u32[]{:S(2)}) collective-permute-start(bf16[144,128]{1,0:T(8,128)(2,1)S(1)} %pad_maximum_fusion.4), channel_id=1, source_target_pairs={{0,128},{16,144},{32,160},{48,176},{64,192},{80,208},{96,224},{112... | collective-permute-start | bytes 110600 | tf_op jit(solution)/shard_map/ppermute | solution.py:172
  34.1 1.1 collective-permute-start.2
  35.6 1.4 %collective-permute-start.4 = (bf16[144,128]{1,0:T(8,128)(2,1)S(1)}, bf16[144,128]{1,0:T(8,128)(2,1)S(1)}, u32[]{:S(2)}, u32[]{:S(2)}) collective-permute-start(bf16[144,128]{1,0:T(8,128)(2,1)S(1)} %pad_maximum_fusion.2), channel_id=1, source_target_pairs={{256,384},{272,400},{288,416},{304,432},{320,448},{336,464},{352,4... | collective-permute-start | bytes 110600 | tf_op jit(solution)/shard_map/ppermute | solution.py:172
  36.2 3.1 %collective-permute-start.3 = (bf16[176,128]{1,0:T(8,128)(2,1)S(1)}, bf16[176,128]{1,0:T(8,128)(2,1)S(1)}, u32[]{:S(2)}, u32[]{:S(2)}) collective-permute-start(bf16[176,128]{1,0:T(8,128)(2,1)S(1)} %fusion.51), channel_id=1, source_target_pairs={{512,640},{528,656},{544,672},{560,688},{576,704},{592,720},{608,7... | collective-permute-start | bytes 135176 | tf_op jit(solution)/shard_map/ppermute | solution.py:172
  37.2 0.7 copy-start.9
  37.2 0.7 copy-start.10
  37.2 2.1 %collective-permute-start.5 = (bf16[144,128]{1,0:T(8,128)(2,1)S(1)}, bf16[144,128]{1,0:T(8,128)(2,1)S(1)}, u32[]{:S(2)}, u32[]{:S(2)}) collective-permute-start(bf16[144,128]{1,0:T(8,128)(2,1)S(1)} %pad_maximum_fusion.1), channel_id=1, source_target_pairs={{384,640},{400,656},{416,672},{432,688},{448,704},{464,720},{480,7... | collective-permute-start | bytes 110600 | tf_op jit(solution)/shard_map/ppermute | solution.py:172
  38.7 2.0 %collective-permute-start.6 = (bf16[144,128]{1,0:T(8,128)(2,1)S(1)}, bf16[144,128]{1,0:T(8,128)(2,1)S(1)}, u32[]{:S(2)}, u32[]{:S(2)}) collective-permute-start(bf16[144,128]{1,0:T(8,128)(2,1)S(1)} %pad_maximum_fusion.1), channel_id=1, source_target_pairs={{384,512},{400,528},{416,544},{432,560},{448,576},{464,592},{480,6... | collective-permute-start | bytes 110600 | tf_op jit(solution)/shard_map/ppermute | solution.py:172
  40.1 0.7 collective-permute-start.7
  40.8 0.7 collective-permute-start.8

commit v6 on v5

--- a/solution.py
+++ b/solution.py
@@ -145,11 +145,13 @@
     first_x, tail_x, first_b, tail_b = (rest[:, 6 + 3 * i : 9 + 3 * i] for i in range(4))
     scale = rest[:, 18:21] + rest[:, 21:24] + rest[:, 24:27]
     shifted = [jnp.pad(v[:-1], ((1, 0), (0, 0), (0, 0))) for v in (tail_x, tail_b)]
-    parts = message[:, :128].astype(f32) + first_update(
+    firsts = first_update(
         own_taps(first_x, taps_x) + tail_taps(shifted[0], taps_x),
         own_taps(first_b, taps_b) + tail_taps(shifted[1], taps_b),
         scale,
     )
+    parts = message[:, :128].astype(f32)
+    parts = [parts[0], *(parts[k] + firsts[k] for k in range(1, NEAR))]
     inside, decays = [jnp.zeros((128, 128), f32)], [jnp.ones((2, 128), f32)]
     after = [jnp.zeros((2, 128), f32), jnp.ones((2, 128), f32)]
     for k in range(NEAR):
@@ -157,11 +159,10 @@
         decays.append(decays[-1] * part_decays[k])
         if k:
             after.append(after[-1] * part_decays[k])
-    total, decay = inside[NEAR], widen(decays[NEAR])
+    base, decay = inside[NEAR], widen(decays[NEAR])
     block = message[NEAR - 1, 128 + 9 : 128 + 18]
     ends = jnp.pad(jnp.concatenate([block[0:3], block[6:9]], axis=0), ((0, 10), (0, 0)))
     known = (own_taps(first_x[0], taps_x), own_taps(first_b[0], taps_b), scale[0])
-    without = first_update(*known)
 
     def change(rows, own_x, own_b, scale):
         x_part, b_part = tail_taps(rows[0:3], taps_x), tail_taps(rows[3:6], taps_b)
@@ -172,14 +173,22 @@
         return lax.ppermute(value, "ctx", pairs)
 
     behind = widen(after[NEAR])
-    base = total - behind * without
+    total = base + behind * firsts[0]
     came = send(jnp.concatenate([total.astype(bf16), ends], axis=0), [(0, 1)]).astype(f32)
     entry, rows = came[:128], came[128:]
     base, known, ends = lax.optimization_barrier((base, known, ends))
+    thirds = [
+        lax.reduce_precision(v, 8, 7)
+        for d in (decays[NEAR], after[NEAR])
+        for v in (d, d - lax.reduce_precision(d, 8, 7))
+    ]
+    extra = (first_x[0], first_b[0], *(rest[0, 18 + 3 * i : 21 + 3 * i] for i in range(3)), *thirds)
     half = len(near) // 2
     for g in range(1, half):
         on = (decay * came[:128] + base + behind * change(came[128:], *known)).astype(bf16)
         sent = jnp.concatenate([on, ends], axis=0)
+        if g == half - 2:
+            sent, extra = lax.optimization_barrier((sent, extra))
         if g < half - 1:
             came = send(sent, [(g, g + 1)])
             if g == 1:
@@ -187,12 +196,6 @@
                 local = make_local(late)
             came = came.astype(f32)
             entry, rows = entry + came[:128], rows + came[128:]
-    thirds = [
-        lax.reduce_precision(v, 8, 7)
-        for d in (decays[NEAR], after[NEAR])
-        for v in (d, d - lax.reduce_precision(d, 8, 7))
-    ]
-    extra = [first_x[0], first_b[0], *(rest[0, 18 + 3 * i : 21 + 3 * i] for i in range(3)), *thirds]
     extra = jnp.concatenate(extra, axis=0).astype(bf16)
     extra = jnp.pad(extra, ((0, 32 - extra.shape[0]), (0, 0)))
     even = jnp.concatenate([base_low, ends, extra], axis=0)
@@ -224,7 +227,7 @@
         entry, rows, far = entry + beside[:128], rows + beside[128:], far + came
         on = (step * came[:128] + own + first_e * change(came[128:], *known_e)).astype(bf16)
     inside = jnp.stack(inside[:NEAR]) + widen(jnp.stack(after[:NEAR])) * (
-        change(rows, *known) - without
+        change(rows, *known)
     )
     decays = widen(jnp.stack(decays[:NEAR]))
     inside, decays, entry = lax.optimization_barrier((inside, decays, entry + base_e))

time: 136 us -> 136 us (level)
  no operation moved by 1% of the time
where the time goes in v6:
time: 136 us
  blocking collectives  92.1 us (68%)
  starting transfers between devices  27 us (20%)
  Pallas kernels  4.81 us (4%)
  local copies, waits for them, and re-layouts  4.38 us (3%)
  matrix products  3.09 us (2%)
  other arithmetic  1.68 us (1%)
  waiting for transfers between devices  1.62 us (1%)
    all_to_all x1, blocking collectives, shards(): lax.all_to_all(normed, 'ctx', split_axis=0, concat_axis=1, tiled=True)  77.6 us
    all_to_all x1, starting transfers between devices, shards(): lax.all_to_all(message, 'ctx', 0, 0, tiled=True, axis_index_groups=near_g...  17.5 us
    all_to_all x1, blocking collectives, entering_states(): lax.all_to_all(states, 'ctx', 0, 0, tiled=True, axis_index_groups=near)  14.6 us
    ppermute x8, starting transfers between devices, send(): return lax.ppermute(value, 'ctx', pairs)  5.93 us
    ppermute x1, starting transfers between devices, halo(): return lax.ppermute(tails, 'ctx', [(i, i + 1) for i in range(count - 1)])  3.53 us
    unnamed x27, local copies, waits for them, and re-layouts  3.08 us
    pallas_call x1, Pallas kernels, shards(): pl.pallas_call(without_halo, out_shape=[shape((width // 128, 128 + EXTRA,...  2.99 us
  transfers between devices with their start and end apart: 10, of which 2 were waited for; matrix products, arithmetic and copies ran while one was open for 2% of the time, Pallas kernels for 1%

profile of v6, /device:TPU:1, one launch (start us, length us, event | category | flops | bytes accessed | tf_op | source)
XLA Modules:
  0.0 135.5 jit_solution(6009875901144902511)
XLA Ops:
  0.0 3.0 %without_halo.1 = (bf16[8,160,128]{2,1,0:T(8,128)(2,1)}, f32[16,128]{1,0:T(8,128)}, f32[16,128]{1,0:T(8,128)}) custom-call(bf16[128,1024]{1,0:T(8,128)(2,1)} %x_ref.3, bf16[128,128]{1,0:T(8,128)(2,1)} %b_ref.3, f32[16,128]{1,0:T(8,128)} %bitcast.350, f32[1,16]{1,0:T(1,128)} %bitcast.351, f32[1,16]{1,0:T(1,128)} %bitcast.352, f32[4,1024]{1,0:T(4,128)} %tx_ref.3, ...), custom_call_target="tpu_custom_call" | custom-call | tf_op jit(solution)/shard_map/without_halo/pallas_call | solution.py:256
  3.0 17.5 %all-to-all-start = ((bf16[8,160,128]{2,1,0:T(8,128)(2,1)}), bf16[8,160,128]{2,1,0:T(8,128)(2,1)S(1)}, u32[]{:S(2)}, u32[]{:S(2)}) async-start(bf16[8,160,128]{2,1,0:T(8,128)(2,1)} %get-tuple-element.56), calls=%async_computation | async-start | bytes 655360 | tf_op jit(solution)/shard_map/all_to_all | solution.py:289
  20.5 1.4 %pack_tails.1 = bf16[16,1280]{1,0:T(8,128)(2,1)} custom-call(bf16[128,1024]{1,0:T(8,128)(2,1)} %x_ref.3, bf16[128,128]{1,0:T(8,128)(2,1)} %b_ref.3, bf16[128,128]{1,0:T(8,128)(2,1)} %c_ref.1), custom_call_target="tpu_custom_call" | custom-call | tf_op jit(solution)/shard_map/pack_tails/pallas_call | solution.py:273
  21.9 3.5 %collective-permute-start = (bf16[16,1280]{1,0:T(8,128)(2,1)}, bf16[16,1280]{1,0:T(8,128)(2,1)S(1)}, u32[]{:S(2)}, u32[]{:S(2)}) collective-permute-start(bf16[16,1280]{1,0:T(8,128)(2,1)} %pack_tails.1), channel_id=1, source_target_pairs={{0,16},{16,32},{32,48},{48,64},{64,80},{80,96},{96,112},{112,128},... | collective-permute-start | bytes 122888 | tf_op jit(solution)/shard_map/ppermute | solution.py:242
  25.5 0.0 copy-start.3
  25.5 0.2 copy.21
  25.7 0.5 copy-done.3
  26.2 0.7 copy-done.4
  26.9 0.1 fusion.51
  27.0 0.1 fusion.9
  27.2 0.5 copy-done.8
  27.7 0.2 broadcast_multiply_fusion
  27.9 0.5 copy-done.7
  28.4 0.3 copy-done
  28.7 0.4 copy-done.5
  29.1 0.4 all_rows.1
  29.5 1.0 all-to-all-done
  30.9 0.3 fusion.62
  31.2 0.1 fusion.23
  31.3 1.3 collective-permute-start.1
  32.6 0.1 fusion.204
  33.1 0.6 collective-permute-done.1
  33.7 0.2 fusion.26
  34.0 0.7 collective-permute-start.2
  34.7 0.2 copy.20
  34.9 0.2 fusion.4
  35.2 0.7 collective-permute-start.4
  35.9 0.2 concatenate.29
  36.1 0.7 collective-permute-start.3
  36.8 0.2 fusion.30
  37.1 0.7 collective-permute-start.5
  37.8 0.8 convolution_add_fusion
  38.6 0.7 collective-permute-start.6
  39.4 0.2 fusion.2
  39.7 0.2 fusion.5
  39.9 0.7 collective-permute-start.7
  40.7 0.7 collective-permute-start.8
  41.5 0.2 fusion.136
  41.7 0.1 fusion.14
  41.8 0.2 fusion
  42.0 0.1 add_convert_fusion
  42.1 14.6 %all_to_all.29 = bf16[8,128,128]{2,1,0:T(8,128)(2,1)S(1)} all-to-all(bf16[8,128,128]{2,1,0:T(8,128)(2,1)S(1)} %add_convert_fusion), channel_id=1, replica_groups={{0,16,32,48,64,80,96,112},{128,144,160,176,192,208,224,240},{256,272,28..., dimensions={0} | all-to-all | bytes 524288 | tf_op jit(solution)/shard_map/all_to_all | solution.py:236
  56.7 0.2 fusion.54
  56.9 0.1 multiply_add_fusion
  57.0 0.2 fusion.13
  57.2 0.1 fusion.11
  57.2 77.6 %all_to_all.30 = bf16[64,16,128]{2,1,0:T(8,128)(2,1)S(1)} all-to-all(bf16[64,16,128]{2,1,0:T(8,128)(2,1)S(1)} %bitcast.335), channel_id=1, replica_groups=mesh['ctx'=64,'tp'=16] {'ctx'}, dimensions={0} | all-to-all | bytes 524288 | tf_op jit(solution)/shard_map/all_to_all | solution.py:310
  134.8 0.7 copy_bitcast_fusion
  (110 shorter events, 1.0 us)
Async XLA Ops:
  3.0 27.5 %all-to-all-start = ((bf16[8,160,128]{2,1,0:T(8,128)(2,1)}), bf16[8,160,128]{2,1,0:T(8,128)(2,1)S(1)}, u32[]{:S(2)}, u32[]{:S(2)}) async-start(bf16[8,160,128]{2,1,0:T(8,128)(2,1)} %get-tuple-element.56), calls=%async_computation | async-start | bytes 655360 | tf_op jit(solution)/shard_map/all_to_all | solution.py:289
  20.5 5.0 %copy-start.6 = (bf16[128,1024]{1,0:T(8,128)(2,1)S(1)}, bf16[128,1024]{1,0:T(8,128)(2,1)}, u32[]{:S(2)}) copy-start(bf16[128,1024]{1,0:T(8,128)(2,1)} %param.13) | copy-start | bytes 786436
  21.9 6.5 %collective-permute-start = (bf16[16,1280]{1,0:T(8,128)(2,1)}, bf16[16,1280]{1,0:T(8,128)(2,1)S(1)}, u32[]{:S(2)}, u32[]{:S(2)}) collective-permute-start(bf16[16,1280]{1,0:T(8,128)(2,1)} %pack_tails.1), channel_id=1, source_target_pairs={{0,16},{16,32},{32,48},{48,64},{64,80},{80,96},{96,112},{112,128},... | collective-permute-start | bytes 122888 | tf_op jit(solution)/shard_map/ppermute | solution.py:242
  25.5 0.7 copy-start.3
  26.2 0.7 copy-start.4
  27.0 0.7 copy-start.8
  27.7 0.7 copy-start.7
  27.7 1.0 copy-start
  27.7 1.0 copy-start.1
  27.7 1.0 copy-start.2
  28.4 0.7 copy-start.5
  31.3 2.3 %collective-permute-start.1 = (bf16[144,128]{1,0:T(8,128)(2,1)S(1)}, bf16[144,128]{1,0:T(8,128)(2,1)S(1)}, u32[]{:S(2)}, u32[]{:S(2)}) collective-permute-start(bf16[144,128]{1,0:T(8,128)(2,1)S(1)} %pad_maximum_fusion.4), channel_id=1, source_target_pairs={{0,128},{16,144},{32,160},{48,176},{64,192},{80,208},{96,224},{112... | collective-permute-start | bytes 110600 | tf_op jit(solution)/shard_map/ppermute | solution.py:173
  34.0 0.9 collective-permute-start.2
  35.2 1.6 %collective-permute-start.4 = (bf16[144,128]{1,0:T(8,128)(2,1)S(1)}, bf16[144,128]{1,0:T(8,128)(2,1)S(1)}, u32[]{:S(2)}, u32[]{:S(2)}) collective-permute-start(bf16[144,128]{1,0:T(8,128)(2,1)S(1)} %pad_maximum_fusion.2), channel_id=1, source_target_pairs={{256,384},{272,400},{288,416},{304,432},{320,448},{336,464},{352,4... | collective-permute-start | bytes 110600 | tf_op jit(solution)/shard_map/ppermute | solution.py:173
  36.1 3.1 %collective-permute-start.3 = (bf16[176,128]{1,0:T(8,128)(2,1)S(1)}, bf16[176,128]{1,0:T(8,128)(2,1)S(1)}, u32[]{:S(2)}, u32[]{:S(2)}) collective-permute-start(bf16[176,128]{1,0:T(8,128)(2,1)S(1)} %fusion.53), channel_id=1, source_target_pairs={{512,640},{528,656},{544,672},{560,688},{576,704},{592,720},{608,7... | collective-permute-start | bytes 135176 | tf_op jit(solution)/shard_map/ppermute | solution.py:173
  37.1 0.7 copy-start.9
  37.1 0.7 copy-start.10
  37.1 2.1 %collective-permute-start.5 = (bf16[144,128]{1,0:T(8,128)(2,1)S(1)}, bf16[144,128]{1,0:T(8,128)(2,1)S(1)}, u32[]{:S(2)}, u32[]{:S(2)}) collective-permute-start(bf16[144,128]{1,0:T(8,128)(2,1)S(1)} %pad_maximum_fusion.1), channel_id=1, source_target_pairs={{384,640},{400,656},{416,672},{432,688},{448,704},{464,720},{480,7... | collective-permute-start | bytes 110600 | tf_op jit(solution)/shard_map/ppermute | solution.py:173
  38.6 2.0 %collective-permute-start.6 = (bf16[144,128]{1,0:T(8,128)(2,1)S(1)}, bf16[144,128]{1,0:T(8,128)(2,1)S(1)}, u32[]{:S(2)}, u32[]{:S(2)}) collective-permute-start(bf16[144,128]{1,0:T(8,128)(2,1)S(1)} %pad_maximum_fusion.1), channel_id=1, source_target_pairs={{384,512},{400,528},{416,544},{432,560},{448,576},{464,592},{480,6... | collective-permute-start | bytes 110600 | tf_op jit(solution)/shard_map/ppermute | solution.py:173
  39.9 0.7 collective-permute-start.7
  40.7 0.7 collective-permute-start.8

commit v7 on v6

--- a/solution.py
+++ b/solution.py
@@ -188,12 +188,12 @@
         on = (decay * came[:128] + base + behind * change(came[128:], *known)).astype(bf16)
         sent = jnp.concatenate([on, ends], axis=0)
         if g == half - 2:
-            sent, extra = lax.optimization_barrier((sent, extra))
+            sent, extra, late = lax.optimization_barrier((sent, extra, late))
+            local = make_local(*late)
         if g < half - 1:
             came = send(sent, [(g, g + 1)])
             if g == 1:
-                base_low, late, came = lax.optimization_barrier((base.astype(bf16), late, came))
-                local = make_local(late)
+                base_low, came = lax.optimization_barrier((base.astype(bf16), came))
             came = came.astype(f32)
             entry, rows = entry + came[:128], rows + came[128:]
     extra = jnp.concatenate(extra, axis=0).astype(bf16)
@@ -288,7 +288,7 @@
     )(tails, late_x, late_b, late_c, conv_x, conv_b, conv_c)
     message = lax.all_to_all(message, "ctx", 0, 0, tiled=True, axis_index_groups=near_groups())
     message, x_act, b_act, c_act = lax.optimization_barrier((message, x_act, b_act, c_act))
-    def make_local(delta):
+    def make_local(delta, x_act):
         lower = jnp.triu(jnp.ones((SPAN, SPAN), dtype=bool))
         x_heads = x_act.T.reshape(heads, head_size, length)
         scores = jnp.dot(b_act, c_act.T, preferred_element_type=f32)
@@ -299,7 +299,7 @@
         gate = jax.nn.silu(z_in.astype(f32)).T
         return inner, gate, gate * norm_gain[:, None], jnp.exp(logs)
 
-    state_low, local = entering_states(message, conv_x, conv_b, delta, make_local)
+    state_low, local = entering_states(message, conv_x, conv_b, (delta, x_act), make_local)
     inner, gate, gain, grown = local
     outer = jnp.dot(state_low, c_act.T, preferred_element_type=f32)
     y_val = inner + grown[:, None, :] * outer.reshape(heads, head_size, length)

time: 136 us -> 136 us (level)
  no operation moved by 1% of the time
where the time goes in v7:
time: 136 us
  blocking collectives  92.1 us (68%)
  starting transfers between devices  27 us (20%)
  Pallas kernels  4.81 us (4%)
  local copies, waits for them, and re-layouts  4.39 us (3%)
  matrix products  3.09 us (2%)
  other arithmetic  1.67 us (1%)
  waiting for transfers between devices  1.62 us (1%)
    all_to_all x1, blocking collectives, shards(): lax.all_to_all(normed, 'ctx', split_axis=0, concat_axis=1, tiled=True)  77.6 us
    all_to_all x1, starting transfers between devices, shards(): lax.all_to_all(message, 'ctx', 0, 0, tiled=True, axis_index_groups=near_g...  17.5 us
    all_to_all x1, blocking collectives, entering_states(): lax.all_to_all(states, 'ctx', 0, 0, tiled=True, axis_index_groups=near)  14.6 us
    ppermute x8, starting transfers between devices, send(): return lax.ppermute(value, 'ctx', pairs)  5.94 us
    ppermute x1, starting transfers between devices, halo(): return lax.ppermute(tails, 'ctx', [(i, i + 1) for i in range(count - 1)])  3.53 us
    unnamed x27, local copies, waits for them, and re-layouts  3.08 us
    pallas_call x1, Pallas kernels, shards(): pl.pallas_call(without_halo, out_shape=[shape((width // 128, 128 + EXTRA,...  2.99 us
  transfers between devices with their start and end apart: 10, of which 2 were waited for; matrix products, arithmetic and copies ran while one was open for 2% of the time, Pallas kernels for 1%

profile of v7, /device:TPU:1, one launch (start us, length us, event | category | flops | bytes accessed | tf_op | source)
XLA Modules:
  0.0 135.5 jit_solution(15849884905183782991)
XLA Ops:
  0.0 3.0 %without_halo.1 = (bf16[8,160,128]{2,1,0:T(8,128)(2,1)}, f32[16,128]{1,0:T(8,128)}, f32[16,128]{1,0:T(8,128)}) custom-call(bf16[128,1024]{1,0:T(8,128)(2,1)} %x_ref.3, bf16[128,128]{1,0:T(8,128)(2,1)} %b_ref.3, f32[16,128]{1,0:T(8,128)} %bitcast.350, f32[1,16]{1,0:T(1,128)} %bitcast.351, f32[1,16]{1,0:T(1,128)} %bitcast.352, f32[4,1024]{1,0:T(4,128)} %tx_ref.3, ...), custom_call_target="tpu_custom_call" | custom-call | tf_op jit(solution)/shard_map/without_halo/pallas_call | solution.py:256
  3.0 17.5 %all-to-all-start = ((bf16[8,160,128]{2,1,0:T(8,128)(2,1)}), bf16[8,160,128]{2,1,0:T(8,128)(2,1)S(1)}, u32[]{:S(2)}, u32[]{:S(2)}) async-start(bf16[8,160,128]{2,1,0:T(8,128)(2,1)} %get-tuple-element.57), calls=%async_computation | async-start | bytes 655360 | tf_op jit(solution)/shard_map/all_to_all | solution.py:289
  20.5 1.4 %pack_tails.1 = bf16[16,1280]{1,0:T(8,128)(2,1)} custom-call(bf16[128,1024]{1,0:T(8,128)(2,1)} %x_ref.3, bf16[128,128]{1,0:T(8,128)(2,1)} %b_ref.3, bf16[128,128]{1,0:T(8,128)(2,1)} %c_ref.1), custom_call_target="tpu_custom_call" | custom-call | tf_op jit(solution)/shard_map/pack_tails/pallas_call | solution.py:273
  21.9 3.5 %collective-permute-start = (bf16[16,1280]{1,0:T(8,128)(2,1)}, bf16[16,1280]{1,0:T(8,128)(2,1)S(1)}, u32[]{:S(2)}, u32[]{:S(2)}) collective-permute-start(bf16[16,1280]{1,0:T(8,128)(2,1)} %pack_tails.1), channel_id=1, source_target_pairs={{0,16},{16,32},{32,48},{48,64},{64,80},{80,96},{96,112},{112,128},... | collective-permute-start | bytes 122888 | tf_op jit(solution)/shard_map/ppermute | solution.py:242
  25.5 0.0 copy-start.3
  25.5 0.2 copy.21
  25.7 0.5 copy-done.3
  26.2 0.7 copy-done.4
  26.9 0.1 fusion.51
  27.0 0.1 fusion.9
  27.2 0.5 copy-done.8
  27.7 0.2 broadcast_multiply_fusion
  27.9 0.5 copy-done.7
  28.4 0.3 copy-done
  28.7 0.4 copy-done.5
  29.1 0.4 all_rows.1
  29.5 1.0 all-to-all-done
  30.9 0.3 fusion.62
  31.2 0.1 fusion.23
  31.3 1.3 collective-permute-start.1
  32.6 0.1 fusion.204
  33.1 0.6 collective-permute-done.1
  33.7 0.2 fusion.26
  34.0 0.7 collective-permute-start.2
  34.8 0.2 fusion.4
  35.0 0.7 collective-permute-start.4
  35.7 0.2 concatenate.29
  35.9 0.2 copy.20
  36.1 0.7 collective-permute-start.3
  36.9 0.2 fusion.30
  37.1 0.0 copy-start.10
  37.1 0.7 collective-permute-start.5
  37.8 0.8 convolution_add_fusion
  38.6 0.7 collective-permute-start.6
  39.4 0.2 fusion.2
  39.7 0.2 fusion.5
  40.0 0.7 collective-permute-start.7
  40.7 0.7 collective-permute-start.8
  41.5 0.2 fusion.136
  41.8 0.2 fusion
  42.1 0.1 add_convert_fusion
  42.1 14.6 %all_to_all.29 = bf16[8,128,128]{2,1,0:T(8,128)(2,1)S(1)} all-to-all(bf16[8,128,128]{2,1,0:T(8,128)(2,1)S(1)} %add_convert_fusion), channel_id=1, replica_groups={{0,16,32,48,64,80,96,112},{128,144,160,176,192,208,224,240},{256,272,28..., dimensions={0} | all-to-all | bytes 524288 | tf_op jit(solution)/shard_map/all_to_all | solution.py:236
  56.7 0.2 fusion.54
  56.9 0.1 multiply_add_fusion
  57.0 0.2 fusion.13
  57.2 0.1 fusion.11
  57.2 77.6 %all_to_all.30 = bf16[64,16,128]{2,1,0:T(8,128)(2,1)S(1)} all-to-all(bf16[64,16,128]{2,1,0:T(8,128)(2,1)S(1)} %bitcast.335), channel_id=1, replica_groups=mesh['ctx'=64,'tp'=16] {'ctx'}, dimensions={0} | all-to-all | bytes 524288 | tf_op jit(solution)/shard_map/all_to_all | solution.py:310
  134.8 0.7 copy_bitcast_fusion
  (110 shorter events, 1.0 us)
Async XLA Ops:
  3.0 27.5 %all-to-all-start = ((bf16[8,160,128]{2,1,0:T(8,128)(2,1)}), bf16[8,160,128]{2,1,0:T(8,128)(2,1)S(1)}, u32[]{:S(2)}, u32[]{:S(2)}) async-start(bf16[8,160,128]{2,1,0:T(8,128)(2,1)} %get-tuple-element.57), calls=%async_computation | async-start | bytes 655360 | tf_op jit(solution)/shard_map/all_to_all | solution.py:289
  20.5 5.0 %copy-start.6 = (bf16[128,1024]{1,0:T(8,128)(2,1)S(1)}, bf16[128,1024]{1,0:T(8,128)(2,1)}, u32[]{:S(2)}) copy-start(bf16[128,1024]{1,0:T(8,128)(2,1)} %param.13) | copy-start | bytes 786436
  21.9 6.5 %collective-permute-start = (bf16[16,1280]{1,0:T(8,128)(2,1)}, bf16[16,1280]{1,0:T(8,128)(2,1)S(1)}, u32[]{:S(2)}, u32[]{:S(2)}) collective-permute-start(bf16[16,1280]{1,0:T(8,128)(2,1)} %pack_tails.1), channel_id=1, source_target_pairs={{0,16},{16,32},{32,48},{48,64},{64,80},{80,96},{96,112},{112,128},... | collective-permute-start | bytes 122888 | tf_op jit(solution)/shard_map/ppermute | solution.py:242
  25.5 0.7 copy-start.3
  26.2 0.7 copy-start.4
  27.0 0.7 copy-start.8
  27.7 0.7 copy-start.7
  27.7 1.0 copy-start
  27.7 1.0 copy-start.1
  27.7 1.0 copy-start.2
  28.4 0.7 copy-start.5
  31.3 2.3 %collective-permute-start.1 = (bf16[144,128]{1,0:T(8,128)(2,1)S(1)}, bf16[144,128]{1,0:T(8,128)(2,1)S(1)}, u32[]{:S(2)}, u32[]{:S(2)}) collective-permute-start(bf16[144,128]{1,0:T(8,128)(2,1)S(1)} %pad_maximum_fusion.4), channel_id=1, source_target_pairs={{0,128},{16,144},{32,160},{48,176},{64,192},{80,208},{96,224},{112... | collective-permute-start | bytes 110600 | tf_op jit(solution)/shard_map/ppermute | solution.py:173
  34.0 0.7 collective-permute-start.2
  35.0 1.8 %collective-permute-start.4 = (bf16[144,128]{1,0:T(8,128)(2,1)S(1)}, bf16[144,128]{1,0:T(8,128)(2,1)S(1)}, u32[]{:S(2)}, u32[]{:S(2)}) collective-permute-start(bf16[144,128]{1,0:T(8,128)(2,1)S(1)} %pad_maximum_fusion.2), channel_id=1, source_target_pairs={{256,384},{272,400},{288,416},{304,432},{320,448},{336,464},{352,4... | collective-permute-start | bytes 110600 | tf_op jit(solution)/shard_map/ppermute | solution.py:173
  36.1 3.1 %collective-permute-start.3 = (bf16[176,128]{1,0:T(8,128)(2,1)S(1)}, bf16[176,128]{1,0:T(8,128)(2,1)S(1)}, u32[]{:S(2)}, u32[]{:S(2)}) collective-permute-start(bf16[176,128]{1,0:T(8,128)(2,1)S(1)} %fusion.53), channel_id=1, source_target_pairs={{512,640},{528,656},{544,672},{560,688},{576,704},{592,720},{608,7... | collective-permute-start | bytes 135176 | tf_op jit(solution)/shard_map/ppermute | solution.py:173
  37.1 0.7 copy-start.9
  37.1 0.7 copy-start.10
  37.1 2.1 %collective-permute-start.5 = (bf16[144,128]{1,0:T(8,128)(2,1)S(1)}, bf16[144,128]{1,0:T(8,128)(2,1)S(1)}, u32[]{:S(2)}, u32[]{:S(2)}) collective-permute-start(bf16[144,128]{1,0:T(8,128)(2,1)S(1)} %pad_maximum_fusion.1), channel_id=1, source_target_pairs={{384,640},{400,656},{416,672},{432,688},{448,704},{464,720},{480,7... | collective-permute-start | bytes 110600 | tf_op jit(solution)/shard_map/ppermute | solution.py:173
  38.6 2.0 %collective-permute-start.6 = (bf16[144,128]{1,0:T(8,128)(2,1)S(1)}, bf16[144,128]{1,0:T(8,128)(2,1)S(1)}, u32[]{:S(2)}, u32[]{:S(2)}) collective-permute-start(bf16[144,128]{1,0:T(8,128)(2,1)S(1)} %pad_maximum_fusion.1), channel_id=1, source_target_pairs={{384,512},{400,528},{416,544},{432,560},{448,576},{464,592},{480,6... | collective-permute-start | bytes 110600 | tf_op jit(solution)/shard_map/ppermute | solution.py:173
  40.0 0.7 collective-permute-start.7
  40.7 0.7 collective-permute-start.8

commit v8 on v7

--- a/solution.py
+++ b/solution.py
@@ -67,6 +67,8 @@
     lane = lax.broadcasted_iota(jnp.int32, (length, 128), 1)
     late = lax.broadcasted_iota(jnp.int32, (length, 128), 0) >= back
     extra[...] = jnp.zeros(extra.shape, jnp.float32)
+    extra[12:15, :] = b_scratch[8:11, :]
+    extra[15:18, :] = b_scratch[5 + length : 8 + length, :]
     for p in range(width // 128):
         here = slice(128 * p, 128 * p + 128)
         x_act = conv_silu(nothing, x_ref[:, here], tx_ref[:, here], scratch)
@@ -81,8 +83,6 @@
             extra[k : k + 1, :] = jnp.broadcast_to(decay[k // 2][h : h + 1, :], (1, 128))
         extra[6:9, :] = scratch[8:11, :]
         extra[9:12, :] = scratch[5 + length : 8 + length, :]
-        extra[12:15, :] = b_scratch[8:11, :]
-        extra[15:18, :] = b_scratch[5 + length : 8 + length, :]
         for k, part in enumerate(split3(factor[0:8])):
             extra[18 + 3 * k : 21 + 3 * k, :] = part.astype(jnp.float32)[0:3]
         message_ref[p, 128 : 128 + EXTRA, :] = extra[...].astype(jnp.bfloat16)

time: 136 us -> 136 us (level)
  no operation moved by 1% of the time
where the time goes in v8:
time: 136 us
  blocking collectives  92.1 us (68%)
  starting transfers between devices  27 us (20%)
  Pallas kernels  4.82 us (4%)
  local copies, waits for them, and re-layouts  4.39 us (3%)
  matrix products  3.1 us (2%)
  other arithmetic  1.67 us (1%)
  waiting for transfers between devices  1.62 us (1%)
    all_to_all x1, blocking collectives, shards(): lax.all_to_all(normed, 'ctx', split_axis=0, concat_axis=1, tiled=True)  77.5 us
    all_to_all x1, starting transfers between devices, shards(): lax.all_to_all(message, 'ctx', 0, 0, tiled=True, axis_index_groups=near_g...  17.5 us
    all_to_all x1, blocking collectives, entering_states(): lax.all_to_all(states, 'ctx', 0, 0, tiled=True, axis_index_groups=near)  14.6 us
    ppermute x8, starting transfers between devices, send(): return lax.ppermute(value, 'ctx', pairs)  5.94 us
    ppermute x1, starting transfers between devices, halo(): return lax.ppermute(tails, 'ctx', [(i, i + 1) for i in range(count - 1)])  3.53 us
    unnamed x27, local copies, waits for them, and re-layouts  3.08 us
    pallas_call x1, Pallas kernels, shards(): pl.pallas_call(without_halo, out_shape=[shape((width // 128, 128 + EXTRA,...  2.99 us
  transfers between devices with their start and end apart: 10, of which 2 were waited for; matrix products, arithmetic and copies ran while one was open for 2% of the time, Pallas kernels for 1%

profile of v8, /device:TPU:1, one launch (start us, length us, event | category | flops | bytes accessed | tf_op | source)
XLA Modules:
  0.0 135.5 jit_solution(17405800022473319626)
XLA Ops:
  0.0 3.0 %without_halo.1 = (bf16[8,160,128]{2,1,0:T(8,128)(2,1)}, f32[16,128]{1,0:T(8,128)}, f32[16,128]{1,0:T(8,128)}) custom-call(bf16[128,1024]{1,0:T(8,128)(2,1)} %x_ref.3, bf16[128,128]{1,0:T(8,128)(2,1)} %b_ref.3, f32[16,128]{1,0:T(8,128)} %bitcast.350, f32[1,16]{1,0:T(1,128)} %bitcast.351, f32[1,16]{1,0:T(1,128)} %bitcast.352, f32[4,1024]{1,0:T(4,128)} %tx_ref.3, ...), custom_call_target="tpu_custom_call" | custom-call | tf_op jit(solution)/shard_map/without_halo/pallas_call | solution.py:256
  3.0 17.5 %all-to-all-start = ((bf16[8,160,128]{2,1,0:T(8,128)(2,1)}), bf16[8,160,128]{2,1,0:T(8,128)(2,1)S(1)}, u32[]{:S(2)}, u32[]{:S(2)}) async-start(bf16[8,160,128]{2,1,0:T(8,128)(2,1)} %get-tuple-element.57), calls=%async_computation | async-start | bytes 655360 | tf_op jit(solution)/shard_map/all_to_all | solution.py:289
  20.5 1.4 %pack_tails.1 = bf16[16,1280]{1,0:T(8,128)(2,1)} custom-call(bf16[128,1024]{1,0:T(8,128)(2,1)} %x_ref.3, bf16[128,128]{1,0:T(8,128)(2,1)} %b_ref.3, bf16[128,128]{1,0:T(8,128)(2,1)} %c_ref.1), custom_call_target="tpu_custom_call" | custom-call | tf_op jit(solution)/shard_map/pack_tails/pallas_call | solution.py:273
  21.9 3.5 %collective-permute-start = (bf16[16,1280]{1,0:T(8,128)(2,1)}, bf16[16,1280]{1,0:T(8,128)(2,1)S(1)}, u32[]{:S(2)}, u32[]{:S(2)}) collective-permute-start(bf16[16,1280]{1,0:T(8,128)(2,1)} %pack_tails.1), channel_id=1, source_target_pairs={{0,16},{16,32},{32,48},{48,64},{64,80},{80,96},{96,112},{112,128},... | collective-permute-start | bytes 122888 | tf_op jit(solution)/shard_map/ppermute | solution.py:242
  25.5 0.0 copy-start.3
  25.5 0.2 copy.21
  25.7 0.5 copy-done.3
  26.2 0.7 copy-done.4
  26.9 0.1 fusion.51
  27.0 0.0 copy-start.8
  27.0 0.1 fusion.9
  27.2 0.5 copy-done.8
  27.7 0.2 broadcast_multiply_fusion
  27.9 0.5 copy-done.7
  28.4 0.3 copy-done
  28.7 0.4 copy-done.5
  29.1 0.4 all_rows.1
  29.5 1.0 all-to-all-done
  30.9 0.3 fusion.62
  31.2 0.1 fusion.23
  31.3 1.3 collective-permute-start.1
  32.6 0.1 fusion.204
  33.1 0.6 collective-permute-done.1
  33.7 0.2 fusion.26
  34.0 0.7 collective-permute-start.2
  34.8 0.2 fusion.4
  35.0 0.7 collective-permute-start.4
  35.7 0.2 concatenate.29
  36.0 0.2 copy.20
  36.1 0.7 collective-permute-start.3
  36.9 0.2 fusion.30
  37.1 0.7 collective-permute-start.5
  37.8 0.8 convolution_add_fusion
  38.6 0.7 collective-permute-start.6
  39.4 0.2 fusion.2
  39.7 0.2 fusion.5
  40.0 0.7 collective-permute-start.7
  40.7 0.7 collective-permute-start.8
  41.5 0.2 fusion.136
  41.8 0.2 fusion
  42.1 0.1 add_convert_fusion
  42.1 14.6 %all_to_all.29 = bf16[8,128,128]{2,1,0:T(8,128)(2,1)S(1)} all-to-all(bf16[8,128,128]{2,1,0:T(8,128)(2,1)S(1)} %add_convert_fusion), channel_id=1, replica_groups={{0,16,32,48,64,80,96,112},{128,144,160,176,192,208,224,240},{256,272,28..., dimensions={0} | all-to-all | bytes 524288 | tf_op jit(solution)/shard_map/all_to_all | solution.py:236
  56.7 0.2 fusion.54
  56.9 0.1 multiply_add_fusion
  57.0 0.2 fusion.13
  57.2 0.1 fusion.11
  57.3 77.5 %all_to_all.30 = bf16[64,16,128]{2,1,0:T(8,128)(2,1)S(1)} all-to-all(bf16[64,16,128]{2,1,0:T(8,128)(2,1)S(1)} %bitcast.335), channel_id=1, replica_groups=mesh['ctx'=64,'tp'=16] {'ctx'}, dimensions={0} | all-to-all | bytes 524288 | tf_op jit(solution)/shard_map/all_to_all | solution.py:310
  134.8 0.7 copy_bitcast_fusion
  (110 shorter events, 1.0 us)
Async XLA Ops:
  3.0 27.5 %all-to-all-start = ((bf16[8,160,128]{2,1,0:T(8,128)(2,1)}), bf16[8,160,128]{2,1,0:T(8,128)(2,1)S(1)}, u32[]{:S(2)}, u32[]{:S(2)}) async-start(bf16[8,160,128]{2,1,0:T(8,128)(2,1)} %get-tuple-element.57), calls=%async_computation | async-start | bytes 655360 | tf_op jit(solution)/shard_map/all_to_all | solution.py:289
  20.5 5.0 %copy-start.6 = (bf16[128,1024]{1,0:T(8,128)(2,1)S(1)}, bf16[128,1024]{1,0:T(8,128)(2,1)}, u32[]{:S(2)}) copy-start(bf16[128,1024]{1,0:T(8,128)(2,1)} %param.13) | copy-start | bytes 786436
  21.9 6.5 %collective-permute-start = (bf16[16,1280]{1,0:T(8,128)(2,1)}, bf16[16,1280]{1,0:T(8,128)(2,1)S(1)}, u32[]{:S(2)}, u32[]{:S(2)}) collective-permute-start(bf16[16,1280]{1,0:T(8,128)(2,1)} %pack_tails.1), channel_id=1, source_target_pairs={{0,16},{16,32},{32,48},{48,64},{64,80},{80,96},{96,112},{112,128},... | collective-permute-start | bytes 122888 | tf_op jit(solution)/shard_map/ppermute | solution.py:242
  25.5 0.7 copy-start.3
  26.2 0.7 copy-start.4
  27.0 0.7 copy-start.8
  27.7 0.7 copy-start.7
  27.7 1.0 copy-start
  27.7 1.0 copy-start.1
  27.7 1.0 copy-start.2
  28.4 0.7 copy-start.5
  31.3 2.3 %collective-permute-start.1 = (bf16[144,128]{1,0:T(8,128)(2,1)S(1)}, bf16[144,128]{1,0:T(8,128)(2,1)S(1)}, u32[]{:S(2)}, u32[]{:S(2)}) collective-permute-start(bf16[144,128]{1,0:T(8,128)(2,1)S(1)} %pad_maximum_fusion.4), channel_id=1, source_target_pairs={{0,128},{16,144},{32,160},{48,176},{64,192},{80,208},{96,224},{112... | collective-permute-start | bytes 110600 | tf_op jit(solution)/shard_map/ppermute | solution.py:173
  34.0 0.7 collective-permute-start.2
  35.0 1.8 %collective-permute-start.4 = (bf16[144,128]{1,0:T(8,128)(2,1)S(1)}, bf16[144,128]{1,0:T(8,128)(2,1)S(1)}, u32[]{:S(2)}, u32[]{:S(2)}) collective-permute-start(bf16[144,128]{1,0:T(8,128)(2,1)S(1)} %pad_maximum_fusion.2), channel_id=1, source_target_pairs={{256,384},{272,400},{288,416},{304,432},{320,448},{336,464},{352,4... | collective-permute-start | bytes 110600 | tf_op jit(solution)/shard_map/ppermute | solution.py:173
  36.1 3.1 %collective-permute-start.3 = (bf16[176,128]{1,0:T(8,128)(2,1)S(1)}, bf16[176,128]{1,0:T(8,128)(2,1)S(1)}, u32[]{:S(2)}, u32[]{:S(2)}) collective-permute-start(bf16[176,128]{1,0:T(8,128)(2,1)S(1)} %fusion.53), channel_id=1, source_target_pairs={{512,640},{528,656},{544,672},{560,688},{576,704},{592,720},{608,7... | collective-permute-start | bytes 135176 | tf_op jit(solution)/shard_map/ppermute | solution.py:173
  37.1 0.7 copy-start.9
  37.1 0.7 copy-start.10
  37.1 2.1 %collective-permute-start.5 = (bf16[144,128]{1,0:T(8,128)(2,1)S(1)}, bf16[144,128]{1,0:T(8,128)(2,1)S(1)}, u32[]{:S(2)}, u32[]{:S(2)}) collective-permute-start(bf16[144,128]{1,0:T(8,128)(2,1)S(1)} %pad_maximum_fusion.1), channel_id=1, source_target_pairs={{384,640},{400,656},{416,672},{432,688},{448,704},{464,720},{480,7... | collective-permute-start | bytes 110600 | tf_op jit(solution)/shard_map/ppermute | solution.py:173
  38.6 2.0 %collective-permute-start.6 = (bf16[144,128]{1,0:T(8,128)(2,1)S(1)}, bf16[144,128]{1,0:T(8,128)(2,1)S(1)}, u32[]{:S(2)}, u32[]{:S(2)}) collective-permute-start(bf16[144,128]{1,0:T(8,128)(2,1)S(1)} %pad_maximum_fusion.1), channel_id=1, source_target_pairs={{384,512},{400,528},{416,544},{432,560},{448,576},{464,592},{480,6... | collective-permute-start | bytes 110600 | tf_op jit(solution)/shard_map/ppermute | solution.py:173
  40.0 0.7 collective-permute-start.7
  40.7 0.7 collective-permute-start.8
